TPU v7x, 256 devices: a whole 4x4x8 slice. The times are simulated.
256 devices in a mesh: row: 32 (over z, x), col: 8 (over y, core).
Axes of the slice: x: 4, y: 4, z: 8, core: 2. Of those that a mesh axis runs over, the one named last changes fastest.
Arguments:
- features: bfloat16 [65536, 256], P(('row', 'col')), may hold values from -6 to 6
- grad_out: bfloat16 [65536, 256], P(('row', 'col')), may hold values from -6 to 6
- degrees: int32 [65536], P(('row', 'col')), may hold values from 1 to 65624, as said below
- w_self: bfloat16 [256, 256], replicated, may hold values from -0.375 to 0.375
- w_neigh: bfloat16 [256, 256], replicated, may hold values from -0.375 to 0.375
- bias: float32 [256], replicated, may hold values from -4 to 4
- tile_slots: int32 [32, 8, 176], P('row', 'col'), may hold values from 0 to 1023, as said below
- tile_count: int32 [32, 8], P('row', 'col'), may hold values from 44 to 176, as said below
- tile_masks: int32 [32, 8, 176, 16, 128], P('row', 'col'), may hold values from 0 to 255
Outputs:
- layer_out: bfloat16 [65536, 256], P(('row', 'col'))
- grad_in: bfloat16 [65536, 256], P(('row', 'col'))
- grad_w_self: float32 [256, 256], replicated
- grad_w_neigh: float32 [256, 256], replicated
Inputs may be any that keep to these rules, and one draw needn't show every extreme that they name: `tile_slots`: on each device the 176 slot numbers are distinct and rise; slot s names block row s % 16 of the device's row group and block column s // 16 of its panel. Only a device's first tile_count tiles are live; the others are ignored. Some device holds 176 live tiles. `degrees`: each node's degree is at least the number of ones in its row of A, and at least 1; some node has the largest degree.
All inputs are finite; a program needn't handle non-finite values.
Results may differ from a plain program's by a relative error of at most 0.014.
Values may be sent and summed in bfloat16 or wider, within the bound.
A program may use at most 64 MiB of HBM per device.

v0:
```python
import math

import jax
import jax.numpy as jnp
from jax import lax
from jax.sharding import PartitionSpec as P

group_tiles = 8


def unpack_tiles(mask_words):
    shifts = jnp.arange(8, dtype=jnp.int32)
    bit_values = jnp.bitwise_and(
        jnp.right_shift(mask_words[:, :, None, :], shifts[None, None, :, None]), 1
    )
    return bit_values.reshape(mask_words.shape[0], mask_words.shape[1] * 8, mask_words.shape[2])


def tile_range(slot_ids, live_count, block_rows, low_column, high_column, tile_width):
    column_block = slot_ids // block_rows
    positions = jnp.arange(slot_ids.shape[0], dtype=jnp.int32)
    is_live = positions < live_count
    first_tile = jnp.sum(
        jnp.logical_and(is_live, (column_block + 1) * tile_width <= low_column).astype(jnp.int32)
    )
    last_tile = jnp.sum(
        jnp.logical_and(is_live, column_block * tile_width < high_column).astype(jnp.int32)
    )
    return (first_tile, last_tile)


def aggregate_piece(totals, panel_piece, first_row, slot_ids, live_count, mask_words):
    tile_width = mask_words.shape[2]
    block_rows = totals.shape[0] // tile_width
    piece_rows = panel_piece.shape[0]
    feature_width = panel_piece.shape[1]
    first_tile, last_tile = tile_range(
        slot_ids, live_count, block_rows, first_row, first_row + piece_rows, tile_width
    )
    margin = jnp.zeros((tile_width, feature_width), panel_piece.dtype)
    padded = jnp.concatenate([margin, panel_piece, margin], axis=0)
    group_count = (last_tile - first_tile + group_tiles - 1) // group_tiles
    within = jnp.arange(group_tiles, dtype=jnp.int32)
    tile_columns = jnp.arange(tile_width, dtype=jnp.int32)

    def aggregate_one_group(group_index, running):
        chosen = first_tile + group_index * group_tiles + within
        in_range = chosen < last_tile
        chosen = jnp.minimum(chosen, slot_ids.shape[0] - 1)
        chosen_slots = slot_ids[chosen]
        row_block = chosen_slots % block_rows
        column_block = chosen_slots // block_rows
        columns = column_block[:, None] * tile_width + tile_columns[None, :]
        keep_mask = in_range[:, None] & (columns >= first_row) & (columns < first_row + piece_rows)
        tile_bits = unpack_tiles(mask_words[chosen]) * keep_mask[:, :, None].astype(jnp.int32)
        offsets = column_block * tile_width - first_row + tile_width
        blocks = jax.vmap(lambda offset: lax.dynamic_slice_in_dim(padded, offset, tile_width, 0))(
            offsets
        )
        products = jnp.einsum(
            "gji,gjf->gif",
            tile_bits.astype(jnp.bfloat16),
            blocks,
            preferred_element_type=jnp.float32,
        )
        shaped = running.reshape(block_rows, tile_width, feature_width)
        return shaped.at[row_block].add(products).reshape(running.shape)

    return lax.fori_loop(0, group_count, aggregate_one_group, totals)


def spread_rows(first_row, row_count, slot_ids, live_count, mask_words, upward_rows):
    tile_width = mask_words.shape[2]
    block_rows = upward_rows.shape[0] // tile_width
    feature_width = upward_rows.shape[1]
    first_tile, last_tile = tile_range(
        slot_ids, live_count, block_rows, first_row, first_row + row_count, tile_width
    )
    first_block = first_row // tile_width
    upward_blocks = upward_rows.reshape(block_rows, tile_width, feature_width)
    group_count = (last_tile - first_tile + group_tiles - 1) // group_tiles
    within = jnp.arange(group_tiles, dtype=jnp.int32)

    def spread_one_group(group_index, running):
        chosen = first_tile + group_index * group_tiles + within
        in_range = chosen < last_tile
        chosen = jnp.minimum(chosen, slot_ids.shape[0] - 1)
        chosen_slots = slot_ids[chosen]
        row_block = chosen_slots % block_rows
        column_block = chosen_slots // block_rows
        tile_bits = unpack_tiles(mask_words[chosen]) * in_range[:, None, None].astype(jnp.int32)
        sources = upward_blocks[row_block]
        products = jnp.einsum(
            "gji,gif->gjf",
            tile_bits.astype(jnp.bfloat16),
            sources,
            preferred_element_type=jnp.float32,
        )
        return running.at[column_block - first_block].add(products)

    initial = jnp.zeros((row_count // tile_width, tile_width, feature_width), jnp.float32)
    partial_value = lax.fori_loop(0, group_count, spread_one_group, initial)
    return partial_value.reshape(row_count, feature_width)


def shards(features, grad_out, degrees, w_self, w_neigh, bias, tile_slots, tile_count, tile_masks):
    slot_ids = tile_slots[0, 0]
    live_count = tile_count[0, 0]
    mask_words = tile_masks[0, 0]
    node_rows, feature_width = features.shape
    group_size = node_rows * lax.axis_size("col")
    initial = jnp.zeros((group_size, feature_width), jnp.float32)
    panel = lax.all_gather(features, "row", axis=0, tiled=True)
    partial_value = aggregate_piece(initial, panel, 0, slot_ids, live_count, mask_words)
    summed = lax.psum_scatter(
        partial_value.astype(jnp.bfloat16), "col", scatter_dimension=0, tiled=True
    ).astype(jnp.float32)
    scale_degree = degrees.astype(jnp.float32)[:, None]
    mean_rows = (summed / scale_degree).astype(jnp.bfloat16)
    preact = jnp.dot(features, w_self, preferred_element_type=jnp.float32)
    preact = preact + jnp.dot(mean_rows, w_neigh, preferred_element_type=jnp.float32) + bias
    sigmoid_values = jax.nn.sigmoid(preact)
    layer_out = (preact * sigmoid_values).astype(jnp.bfloat16)
    grad_preact = (
        grad_out.astype(jnp.float32) * sigmoid_values * (1.0 + preact * (1.0 - sigmoid_values))
    ).astype(jnp.bfloat16)
    contract_rows = (((0,), (0,)), ((), ()))
    contract_cols = (((1,), (1,)), ((), ()))
    grad_self = lax.dot_general(
        features, grad_preact, contract_rows, preferred_element_type=jnp.float32
    )
    grad_neigh = lax.dot_general(
        mean_rows, grad_preact, contract_rows, preferred_element_type=jnp.float32
    )
    grad_self, grad_neigh = lax.psum((grad_self, grad_neigh), ("row", "col"))
    grad_scale = 1.0 / math.sqrt(node_rows * lax.axis_size("row") * lax.axis_size("col"))
    upward = lax.dot_general(
        grad_preact, w_neigh, contract_cols, preferred_element_type=jnp.float32
    )
    upward = (upward / scale_degree).astype(jnp.bfloat16)
    upward_rows = lax.all_gather(upward, "col", axis=0, tiled=True)
    panel_size = node_rows * lax.axis_size("row")
    neighbor_grad = lax.psum_scatter(
        spread_rows(0, panel_size, slot_ids, live_count, mask_words, upward_rows).astype(
            jnp.bfloat16
        ),
        "row",
        scatter_dimension=0,
        tiled=True,
    ).astype(jnp.float32)
    self_grad = lax.dot_general(
        grad_preact, w_self, contract_cols, preferred_element_type=jnp.float32
    )
    grad_in = (self_grad + neighbor_grad).astype(jnp.bfloat16)
    return (layer_out, grad_in, grad_self * grad_scale, grad_neigh * grad_scale)


def solution(mesh):
    placed = (
        P(("row", "col"), None),
        P(("row", "col"), None),
        P(("row", "col")),
        P(),
        P(),
        P(),
        P("row", "col", None),
        P("row", "col"),
        P("row", "col", None, None, None),
    )
    return jax.shard_map(
        shards,
        mesh=mesh,
        in_specs=placed,
        out_specs=(P(("row", "col"), None), P(("row", "col"), None), P(), P()),
        check_vma=False,
    )
```

profile of v0, /device:TPU:8, one launch (start us, length us, event | category | flops | bytes accessed | tf_op | source)
XLA Modules:
  0.0 1297.7 jit_solution(11143509822227308921)
XLA Ops:
  11.3 84.0 %all-gather.3.cloned.1.call-done = bf16[8192,256]{1,0:T(8,128)(2,1)} async-done(((bf16[256,256]{1,0:T(8,128)(2,1)}), bf16[8192,256]{1,0:T(8,128)(2,1)}) %all-gather.3.cloned.1.call-update) | async-done | bytes 4194320 | tf_op jit(solution)/shard_map/all_gather | solution.py:113
  95.3 9.5 pad_maximum_fusion
  104.9 174.9 %while.30 = (s32[]{:T(128)}, f32[2048,256]{1,0:T(8,128)S(1)}, s32[]{:T(128)}, s32[]{:T(128)}, s32[176]{0:T(256)S(1)}, /*index=5*/s32[176,16,128]{2,1,0:T(8,128)}...) while((s32[]{:T(128)}, f32[2048,256]{1,0:T(8,128)S(1)}, ...), condition=%wide.region_4.5_spmd.clone, body=%wide.region_2.4_spmd.clone.sunk | while | flops 67902872 | bytes 5061962 | solution.py:69
  106.3 22.1 %while.32 = (s32[]{:T(128)}, bf16[8448,256]{1,0:T(8,128)(2,1)}, s32[8,2]{0,1:T(2,128)S(1)}, bf16[8,128,256]{2,1,0:T(8,128)(2,1)}, s32[]{:T(128)}) while((s32[]{:T(128)}, bf16[8448,256]{1,0:T(8,128)(2,1)}, s32[8,2]{0,1:T(2,128)S(1)}, bf16[8,128,256]{2,1,0:T(8,128)(2,1)}, s32[]{:T(128)}) %tuple.84), condition=%wide.while_cond, body=%wide.while_body.sunk | while | flops 2 | bytes 131685 | solution.py:57
  109.7 2.2 bitcast_dynamic-update-slice_fusion.2
  112.5 2.2 bitcast_dynamic-update-slice_fusion.2
  115.2 2.2 bitcast_dynamic-update-slice_fusion.2
  123.5 2.2 bitcast_dynamic-update-slice_fusion.2
  126.3 2.2 bitcast_dynamic-update-slice_fusion.2
  135.5 22.1 %while.32 = (s32[]{:T(128)}, bf16[8448,256]{1,0:T(8,128)(2,1)}, s32[8,2]{0,1:T(2,128)S(1)}, bf16[8,128,256]{2,1,0:T(8,128)(2,1)}, s32[]{:T(128)}) while((s32[]{:T(128)}, bf16[8448,256]{1,0:T(8,128)(2,1)}, s32[8,2]{0,1:T(2,128)S(1)}, bf16[8,128,256]{2,1,0:T(8,128)(2,1)}, s32[]{:T(128)}) %tuple.84), condition=%wide.while_cond, body=%wide.while_body.sunk | while | flops 2 | bytes 131685 | solution.py:57
  138.8 2.2 bitcast_dynamic-update-slice_fusion.2
  141.6 2.2 bitcast_dynamic-update-slice_fusion.2
  144.4 2.2 bitcast_dynamic-update-slice_fusion.2
  152.6 2.2 bitcast_dynamic-update-slice_fusion.2
  155.4 2.2 bitcast_dynamic-update-slice_fusion.2
  164.6 22.1 %while.32 = (s32[]{:T(128)}, bf16[8448,256]{1,0:T(8,128)(2,1)}, s32[8,2]{0,1:T(2,128)S(1)}, bf16[8,128,256]{2,1,0:T(8,128)(2,1)}, s32[]{:T(128)}) while((s32[]{:T(128)}, bf16[8448,256]{1,0:T(8,128)(2,1)}, s32[8,2]{0,1:T(2,128)S(1)}, bf16[8,128,256]{2,1,0:T(8,128)(2,1)}, s32[]{:T(128)}) %tuple.84), condition=%wide.while_cond, body=%wide.while_body.sunk | while | flops 2 | bytes 131685 | solution.py:57
  168.0 2.2 bitcast_dynamic-update-slice_fusion.2
  170.8 2.2 bitcast_dynamic-update-slice_fusion.2
  173.5 2.2 bitcast_dynamic-update-slice_fusion.2
  181.8 2.2 bitcast_dynamic-update-slice_fusion.2
  193.8 22.1 %while.32 = (s32[]{:T(128)}, bf16[8448,256]{1,0:T(8,128)(2,1)}, s32[8,2]{0,1:T(2,128)S(1)}, bf16[8,128,256]{2,1,0:T(8,128)(2,1)}, s32[]{:T(128)}) while((s32[]{:T(128)}, bf16[8448,256]{1,0:T(8,128)(2,1)}, s32[8,2]{0,1:T(2,128)S(1)}, bf16[8,128,256]{2,1,0:T(8,128)(2,1)}, s32[]{:T(128)}) %tuple.84), condition=%wide.while_cond, body=%wide.while_body.sunk | while | flops 2 | bytes 131685 | solution.py:57
  197.1 2.2 bitcast_dynamic-update-slice_fusion.2
  199.9 2.2 bitcast_dynamic-update-slice_fusion.2
  202.6 2.2 bitcast_dynamic-update-slice_fusion.2
  210.9 2.2 bitcast_dynamic-update-slice_fusion.2
  222.9 22.1 %while.32 = (s32[]{:T(128)}, bf16[8448,256]{1,0:T(8,128)(2,1)}, s32[8,2]{0,1:T(2,128)S(1)}, bf16[8,128,256]{2,1,0:T(8,128)(2,1)}, s32[]{:T(128)}) while((s32[]{:T(128)}, bf16[8448,256]{1,0:T(8,128)(2,1)}, s32[8,2]{0,1:T(2,128)S(1)}, bf16[8,128,256]{2,1,0:T(8,128)(2,1)}, s32[]{:T(128)}) %tuple.84), condition=%wide.while_cond, body=%wide.while_body.sunk | while | flops 2 | bytes 131685 | solution.py:57
  226.3 2.2 bitcast_dynamic-update-slice_fusion.2
  229.0 2.2 bitcast_dynamic-update-slice_fusion.2
  231.8 2.2 bitcast_dynamic-update-slice_fusion.2
  240.1 2.2 bitcast_dynamic-update-slice_fusion.2
  252.1 22.1 %while.32 = (s32[]{:T(128)}, bf16[8448,256]{1,0:T(8,128)(2,1)}, s32[8,2]{0,1:T(2,128)S(1)}, bf16[8,128,256]{2,1,0:T(8,128)(2,1)}, s32[]{:T(128)}) while((s32[]{:T(128)}, bf16[8448,256]{1,0:T(8,128)(2,1)}, s32[8,2]{0,1:T(2,128)S(1)}, bf16[8,128,256]{2,1,0:T(8,128)(2,1)}, s32[]{:T(128)}) %tuple.84), condition=%wide.while_cond, body=%wide.while_body.sunk | while | flops 2 | bytes 131685 | solution.py:57
  255.4 2.2 bitcast_dynamic-update-slice_fusion.2
  258.2 2.2 bitcast_dynamic-update-slice_fusion.2
  260.9 2.2 bitcast_dynamic-update-slice_fusion.2
  269.2 2.2 bitcast_dynamic-update-slice_fusion.2
  282.1 494.0 %reduce-scatter.3.cloned.1.call-done = bf16[256,256]{1,0:T(8,128)(2,1)} async-done(((bf16[2048,256]{1,0:T(8,128)(2,1)}), bf16[256,256]{1,0:T(8,128)(2,1)}) %reduce-scatter.3.cloned.1.call-update) | async-done | bytes 131088 | tf_op jit(solution)/shard_map/reduce_scatter | solution.py:115
  781.0 24.3 %all-gather.5.cloned.1.call-done = bf16[2048,256]{1,0:T(8,128)(2,1)} async-done(((bf16[256,256]{1,0:T(8,128)(2,1)}), bf16[2048,256]{1,0:T(8,128)(2,1)}) %all-gather.5.cloned.1.call-update) | async-done | bytes 1048592 | tf_op jit(solution)/shard_map/all_gather | solution.py:141
  805.4 4.3 broadcast_in_dim.8
  809.6 48.7 %while.31 = (s32[]{:T(128)}, f32[64,128,256]{2,1,0:T(8,128)}, s32[]{:T(128)}, s32[]{:T(128)}, s32[176]{0:T(256)S(1)}, /*index=5*/s32[176,16,128]{2,1,0:T(8,128)}...) while((s32[]{:T(128)}, f32[64,128,256]{2,1,0:T(8,128)}, s32[]{:T(128)}, ...), condition=%wide.region_8.9_spmd.clone, body=%wide.region_6.8_spmd.clone.sunk | while | flops 67897608 | bytes 5974609 | solution.py:102
  814.6 3.1 scatter_fusion
  822.7 3.2 scatter_fusion
  830.8 3.1 scatter_fusion
  838.9 3.1 scatter_fusion
  847.0 3.2 scatter_fusion
  855.1 3.2 scatter_fusion
  858.4 6.0 convert_element_type.88
  864.4 201.2 %all-reduce.4.cloned.1.call-done = (f32[256,256]{0,1:T(8,128)}, f32[256,256]{0,1:T(8,128)}) async-done(((f32[256,256]{0,1:T(8,128)}, f32[256,256]{0,1:T(8,128)}), (f32[256,256]{0,1:T(8,128)}, f32[256,256]{0,1:T(8,128)})) %all-reduce.4.cloned.1.call-update) | async-done | bytes 524304 | tf_op jit(solution)/shard_map/psum | solution.py:135
  1068.3 221.1 %reduce-scatter.5.cloned.1.call-done = bf16[256,256]{1,0:T(8,128)(2,1)} async-done(((bf16[8192,256]{1,0:T(8,128)(2,1)}), bf16[256,256]{1,0:T(8,128)(2,1)}) %reduce-scatter.5.cloned.1.call-update) | async-done | bytes 131088 | tf_op jit(solution)/shard_map/reduce_scatter | solution.py:143
  (310 shorter events, 153.4 us)
Async XLA Ops:
  7.2 769.0 %copy-start = (bf16[256,256]{1,0:T(8,128)(2,1)S(1)}, bf16[256,256]{1,0:T(8,128)(2,1)}, u32[]{:S(2)}) copy-start(bf16[256,256]{1,0:T(8,128)(2,1)} %param.17) | copy-start | bytes 393220
  7.2 88.1 %all-gather.3.cloned.1.call-start = ((), (), s32[]{:S(2)}) async-start(), calls=%async_computation.2 | async-start | bytes 4325376 | tf_op jit(solution)/shard_map/all_gather | solution.py:113
  7.9 768.2 %reduce-scatter.3.cloned.1.call-start = ((), (), s32[]{:S(2)}) async-start(), calls=%async_computation.3 | async-start | bytes 1179648 | tf_op jit(solution)/shard_map/reduce_scatter | solution.py:115
  95.3 9.6 copy-start.1
  104.9 176.1 %copy-start.5 = (s32[256]{0:T(256)S(1)}, s32[256]{0:T(256)}, u32[]{:S(2)}) copy-start(s32[256]{0:T(256)} %param.15) | copy-start | bytes 3076
  104.9 176.1 %copy-start.3 = (bf16[256,256]{1,0:T(8,128)(2,1)S(1)}, bf16[256,256]{1,0:T(8,128)(2,1)}, u32[]{:S(2)}) copy-start(bf16[256,256]{1,0:T(8,128)(2,1)} %param.13) | copy-start | bytes 393220
  279.8 496.3 %copy-start.6 = (bf16[256,256]{1,0:T(8,128)(2,1)S(1)}, bf16[256,256]{1,0:T(8,128)(2,1)}, u32[]{:S(2)}) copy-start(bf16[256,256]{1,0:T(8,128)(2,1)} %param.14) | copy-start | bytes 393220
  279.9 496.3 %copy-start.8 = (f32[256]{0:T(256)S(1)}, f32[256]{0:T(256)}, u32[]{:S(2)}) copy-start(f32[256]{0:T(256)} %param.18) | copy-start | bytes 3076
  281.0 524.4 %all-gather.5.cloned.1.call-start = ((), (), s32[]{:S(2)}) async-start(), calls=%async_computation.4 | async-start | bytes 1179648 | tf_op jit(solution)/shard_map/all_gather | solution.py:141
  776.1 3.9 copy-start.7
  779.0 286.6 %all-reduce.4.cloned.1.call-start = ((), (), s32[]{:S(2)}) async-start(), calls=%async_computation.6 | async-start | bytes 1048576 | tf_op jit(solution)/shard_map/psum | solution.py:135
  781.0 508.4 %reduce-scatter.5.cloned.1.call-start = ((), (), s32[]{:S(2)}) async-start(), calls=%async_computation.5 | async-start | bytes 4325376 | tf_op jit(solution)/shard_map/reduce_scatter | solution.py:143
  805.4 4.3 copy-start.2
  864.4 425.0 %copy-start.4 = (bf16[256,256]{1,0:T(8,128)(2,1)S(1)}, bf16[256,256]{1,0:T(8,128)(2,1)}, u32[]{:S(2)}) copy-start(bf16[256,256]{1,0:T(8,128)(2,1)} %param.16) | copy-start | bytes 393220
Sparse Core Ops, SparseCore 0:
  10.6 84.6 all-gather.2
  281.1 494.9 reduce-scatter.2
  779.1 26.2 all-gather.4
  811.4 254.1 all-reduce.3
  1069.3 220.0 reduce-scatter.4
where the time goes:
time: 1310 us; the launch traced here: 1300 us
  waiting for transfers between devices  1030 us (79%)
  local copies, waits for them, and re-layouts  174 us (13%)
  other arithmetic  54.6 us (4%)
  matrix products  19.3 us (1%)
  between operations  15.8 us (1%)
    reduce_scatter x1, waiting for transfers between devices, shards(): lax.psum_scatter(partial_value.astype(jnp.bfloat16), 'col', scatter_dimen...  494 us
    reduce_scatter x1, waiting for transfers between devices, shards(): lax.psum_scatter(spread_rows(0, panel_size, slot_ids, live_count, mask_wo...  221 us
    psum x1, waiting for transfers between devices, shards(): grad_self, grad_neigh = lax.psum((grad_self, grad_neigh), ('row', 'col'))  201 us
    gather x144, local copies, waits for them, and re-layouts  132 us
    all_gather x1, waiting for transfers between devices, shards(): panel = lax.all_gather(features, 'row', axis=0, tiled=True)  84 us
  transfers between devices with their start and end apart: 5, of which 5 were waited for; matrix products, arithmetic and copies ran while one was open for 5% of the time, Pallas kernels for 0%

commit v1 on v0

v1 whole, which is shorter than its diff:
```python
import functools
import heapq
import math

import jax
import jax.numpy as jnp
from jax import lax
from jax.experimental import pallas as pl
from jax.experimental.pallas import tpu as pltpu
from jax.sharding import PartitionSpec as P

MESH = pl.DeviceIdType.MESH
SMEM = pl.BlockSpec(memory_space=pltpu.SMEM)
VMEM = pl.BlockSpec(memory_space=pltpu.VMEM)
ANY = pl.BlockSpec(memory_space=pl.ANY)
TILE = 128
UNROLL = 16
VMEM_BYTES = 60 << 20


def torus_plan(nx, nz, split, latency=1.0, rate=0.01):
    size = {"x": nx, "z": nz}
    transfers, entries, order = [], {}, []
    free, heap = {}, []

    def wrap(d, n):
        d %= n
        return d - n if d > n // 2 else d

    def send(now, node, axis, sign, first, count):
        offset = {"x": node[1], "z": node[2]}
        offset[axis] = wrap(offset[axis] - sign, size[axis])
        index = len(transfers)
        transfers.append((axis, sign, first, count, (node[0], offset["x"], offset["z"])))
        start = max(now, free.get((axis, sign), 0.0))
        free[axis, sign] = start + count * rate
        heapq.heappush(heap, (free[axis, sign] + latency, index))
        entries[node][1].append(index)

    def forward(now, node):
        part = node[0]
        begin, full = (0, split[0]) if part == 0 else (split[0], split[1])
        offset = {"x": node[1], "z": node[2]}
        p, q = ("x", "z") if part == 0 else ("z", "x")
        dp, dq = offset[p], offset[q]
        half_p, half_q = size[p] // 2, size[q] // 2
        lower = (full // 2 + 15) // 16 * 16
        for sign in (1, -1):
            if dq == 0 and (dp == 0 or -dp * sign > 0) and dp != half_p:
                if abs(dp) + 1 < half_p:
                    send(now, node, p, sign, begin, full)
                elif sign == 1:
                    send(now, node, p, sign, begin, lower)
                else:
                    send(now, node, p, sign, begin + lower, full - lower)
        for sign in (1, -1):
            if (dq == 0 or -dq * sign > 0) and dq != half_q:
                if abs(dq) + 1 < half_q or (0 <= dp < half_p) == (sign == 1):
                    send(now, node, q, sign, begin, full)

    got = {}
    for part in (0, 1):
        entries[part, 0, 0] = ([], [])
        order.append((part, 0, 0))
        forward(0.0, (part, 0, 0))
    while heap:
        now, index = heapq.heappop(heap)
        count, node = transfers[index][3:]
        entries.setdefault(node, ([], []))[0].append(index)
        got[node] = got.get(node, 0) + count
        if got[node] == split[node[0]]:
            order.append(node)
            forward(now, node)
    return transfers, [(node, *entries[node]) for node in order]


class Torus:
    def __init__(self, nx, nz):
        self.nx, self.nz = nx, nz
        row = lax.axis_index("row")
        self.x, self.z = lax.rem(row, nx), lax.div(row, nx)

    def row(self, dx, dz):
        x = lax.rem(self.x + (dx + self.nx), self.nx)
        z = lax.rem(self.z + (dz + self.nz), self.nz)
        return z * self.nx + x

    def neighbour(self, axis, sign):
        return {"row": self.row(sign, 0) if axis == "x" else self.row(0, sign)}


def greet(barrier, peers):
    for peer in peers:
        pl.semaphore_signal(barrier, inc=1, device_id=peer, device_id_type=MESH)


def row_order(size):
    place = lax.broadcasted_iota(jnp.int32, (size, size), 0)
    node = lax.broadcasted_iota(jnp.int32, (size, size), 1)
    within = place & (TILE - 1)
    source = (place - within) + ((within & 15) << 3) + (within >> 4)
    return jnp.where(source == node, 1.0, 0.0).astype(jnp.bfloat16)


def gather_kernel(transfers, order, nx, nz, features, panel, own, local_sem, send_sem, recv_sem):
    torus = Torus(nx, nz)
    me = torus.row(0, 0)
    barrier = pltpu.get_barrier_semaphore()
    around = [torus.neighbour(axis, sign) for axis in "xz" for sign in (1, -1)]
    greet(barrier, around)
    own[...] = jnp.dot(
        row_order(own.shape[0]), features[...], preferred_element_type=jnp.float32
    ).astype(own.dtype)
    pl.semaphore_wait(barrier, len(around))

    def copy(index, node, source):
        axis, sign, first, count, _ = transfers[index]
        origin = torus.row(node[1], node[2])
        rows = pl.ds(first, count)
        return pltpu.make_async_remote_copy(
            src_ref=own.at[rows] if source else panel.at[origin, rows],
            dst_ref=panel.at[origin, rows],
            send_sem=send_sem.at[index],
            recv_sem=recv_sem.at[index],
            device_id=torus.neighbour(axis, sign),
            device_id_type=MESH,
        )

    started = []
    for node, brought, carried in order:
        for index in brought:
            copy(index, node, False).wait_recv()
        for index in carried:
            started.append(copy(index, node, not brought))
            started[-1].start()
    keep = pltpu.make_async_copy(own, panel.at[me], local_sem)
    keep.start()
    for each in started:
        each.wait_send()
    keep.wait()


def unpack(words):
    return jnp.concatenate(
        [((words >> bit) & 1).astype(jnp.float32).astype(jnp.bfloat16) for bit in range(8)], axis=0
    )


def each_tile(slots, live, masks, block_rows, step):
    last = masks.shape[0] - 1

    def group(index, _):
        for u in range(UNROLL):
            tile = index * UNROLL + u
            held = jnp.minimum(tile, last)
            slot = slots[held]
            words = jnp.where(tile < live, masks[held], 0)
            step(lax.rem(slot, block_rows), lax.div(slot, block_rows), unpack(words))
        return 0

    lax.fori_loop(0, lax.div(live + (UNROLL - 1), UNROLL), group, 0)


def set_zero(total):
    def one(i, _):
        total[i] = jnp.zeros(total.shape[1:], total.dtype)
        return 0

    lax.fori_loop(0, total.shape[0], one, 0)


def round_to(out, total):
    def one(i, _):
        out[i] = total[i].astype(out.dtype)
        return 0

    lax.fori_loop(0, total.shape[0], one, 0)


def aggregate_kernel(slots, count, masks, panel, out, total):
    set_zero(total)

    def step(row_block, column_block, bits):
        total[row_block] += lax.dot_general(
            bits, panel[column_block], (((0,), (0,)), ((), ())), preferred_element_type=jnp.float32
        )

    each_tile(slots, count[0], masks, out.shape[0], step)
    round_to(out, total)


def spread_kernel(slots, count, masks, upward, out, total):
    set_zero(total)

    def step(row_block, column_block, bits):
        total[column_block] += jnp.dot(bits, upward[row_block], preferred_element_type=jnp.float32)

    each_tile(slots, count[0], masks, upward.shape[0], step)
    round_to(out, total)


def middle_kernel(
    n_col, partial, features, grad_out, degrees, w_self, w_neigh, bias,
    layer_out, grad_preact, upward_rows, grad_sums,
    arrived, upward, weight_parts, weight_arrived,
    local_sem, sum_send, sum_recv, up_send, up_recv, weight_send, weight_recv,
):
    col = lax.axis_index("col")
    peers = [lax.rem(col + k, n_col) for k in range(n_col)]
    barrier = pltpu.get_barrier_semaphore()
    greet(barrier, [{"col": peer} for peer in peers[1:]])
    size, width = features.shape
    scale = jnp.broadcast_to(degrees[...].astype(jnp.float32), (width, size)).T
    own_part = jnp.dot(features[...], w_self[...], preferred_element_type=jnp.float32)
    pl.semaphore_wait(barrier, n_col - 1)

    def remote(source, target, sends, recvs, k):
        return pltpu.make_async_remote_copy(
            src_ref=source,
            dst_ref=target,
            send_sem=sends.at[k - 1],
            recv_sem=recvs.at[k - 1],
            device_id={"col": peers[k]},
            device_id_type=MESH,
        )

    started = []
    for k in range(1, n_col):
        started.append(remote(partial.at[peers[k]], arrived.at[k - 1], sum_send, sum_recv, k))
        started[-1].start()
    summed = partial[col].astype(jnp.float32)
    for k in range(1, n_col):
        started[k - 1].wait_recv()
        summed = summed + arrived[k - 1].astype(jnp.float32)
    mean_rows = (summed / scale).astype(jnp.bfloat16)
    preact = own_part + jnp.dot(mean_rows, w_neigh[...], preferred_element_type=jnp.float32)
    preact = preact + bias[...]
    sigmoid_values = jax.nn.sigmoid(preact)
    layer_out[...] = (preact * sigmoid_values).astype(layer_out.dtype)
    gradient = (
        grad_out[...].astype(jnp.float32) * sigmoid_values * (1.0 + preact * (1.0 - sigmoid_values))
    ).astype(jnp.bfloat16)
    grad_preact[...] = gradient
    sent_up = lax.dot_general(
        gradient, w_neigh[...], (((1,), (1,)), ((), ())), preferred_element_type=jnp.float32
    )
    upward[...] = (sent_up / scale).astype(upward.dtype)
    first_up = len(started)
    for k in range(1, n_col):
        started.append(remote(upward, upward_rows.at[col], up_send, up_recv, k))
        started[-1].start()
    keep = pltpu.make_async_copy(upward, upward_rows.at[col], local_sem)
    keep.start()

    contract_rows = (((0,), (0,)), ((), ()))
    rows = width // n_col
    for half, source in enumerate((features[...], mean_rows)):
        product = lax.dot_general(source, gradient, contract_rows, preferred_element_type=jnp.float32)
        product = product.astype(weight_parts.dtype)
        for c in range(n_col):
            weight_parts[c, half * rows : (half + 1) * rows] = product[c * rows : (c + 1) * rows]
    first_weight = len(started)
    for k in range(1, n_col):
        started.append(
            remote(weight_parts.at[peers[k]], weight_arrived.at[k - 1], weight_send, weight_recv, k)
        )
        started[-1].start()
    total = weight_parts[col].astype(jnp.float32)
    for k in range(1, n_col):
        started[first_weight + k - 1].wait_recv()
        total = total + weight_arrived[k - 1].astype(jnp.float32)
    grad_sums[...] = total
    for k in range(1, n_col):
        started[first_up + k - 1].wait_recv()
    for each in started:
        each.wait_send()
    keep.wait()


def scatter_kernel(
    transfers, order, nx, nz, n_col, grad_scale, partial, grad_preact, w_self, grad_sums,
    grad_in, grad_self, grad_neigh,
    total, arrived, z_arrived, x_sums, z_sums, all_sums,
    load_sem, send_sem, recv_sem, z_send, z_recv, x_send, x_recv, zz_send, zz_recv, col_send, col_recv,
):
    torus = Torus(nx, nz)
    col = lax.axis_index("col")
    load = pltpu.make_async_copy(partial, total, load_sem)
    load.start()
    barrier = pltpu.get_barrier_semaphore()
    along_z = [{"row": torus.row(0, k)} for k in range(1, nz)]
    along_x = [{"row": torus.row(k, 0)} for k in range(1, nx)]
    along_col = [{"col": lax.rem(col + k, n_col)} for k in range(1, n_col)]
    greet(barrier, along_z + along_x + along_col)
    moved = jnp.dot(
        row_order(grad_preact.shape[0]), grad_preact[...], preferred_element_type=jnp.float32
    ).astype(jnp.bfloat16)
    self_grad = lax.dot_general(
        moved, w_self[...], (((1,), (1,)), ((), ())), preferred_element_type=jnp.float32
    )
    pl.semaphore_wait(barrier, len(along_z) + len(along_x) + len(along_col))

    started = []

    def start(source, target, sends, recvs, k, peer):
        started.append(
            pltpu.make_async_remote_copy(
                src_ref=source,
                dst_ref=target,
                send_sem=sends.at[k],
                recv_sem=recvs.at[k],
                device_id=peer,
                device_id_type=MESH,
            )
        )
        started[-1].start()
        return started[-1]

    def reduce_along_z():
        return [
            start(grad_sums.at[lax.rem(torus.z + k, nz)], z_arrived.at[k - 1], z_send, z_recv, k - 1, peer)
            for k, peer in enumerate(along_z, 1)
        ]

    def reduce_along_x(before):
        for each in before:
            each.wait_recv()
        part = grad_sums[torus.z]
        for k in range(nz - 1):
            part = part + z_arrived[k]
        x_sums[torus.x] = part
        return [
            start(x_sums.at[torus.x], x_sums.at[torus.x], x_send, x_recv, k, peer)
            for k, peer in enumerate(along_x)
        ]

    def gather_along_z(before):
        for each in before:
            each.wait_recv()
        part = x_sums[0]
        for k in range(1, nx):
            part = part + x_sums[k]
        z_sums[torus.z] = part * grad_scale
        return [
            start(z_sums.at[torus.z], z_sums.at[torus.z], zz_send, zz_recv, k, peer)
            for k, peer in enumerate(along_z)
        ]

    def gather_along_col(before):
        for each in before:
            each.wait_recv()
        all_sums[col] = z_sums[...].reshape(all_sums.shape[1:])
        return [
            start(all_sums.at[col], all_sums.at[col], col_send, col_recv, k, peer)
            for k, peer in enumerate(along_col)
        ]

    def copy(index, node):
        axis, sign, first, count, _ = transfers[index]
        return start(
            total.at[torus.row(node[1], node[2]), pl.ds(first, count)],
            arrived.at[index, pl.ds(0, count)],
            send_sem,
            recv_sem,
            index,
            torus.neighbour(axis, -sign),
        )

    sent = {}
    pending = reduce_along_z()
    stages = {24: reduce_along_x, 36: gather_along_z, 48: gather_along_col}
    load.wait()
    for position, (node, brought, carried) in enumerate(reversed(order)):
        if position in stages:
            pending = stages[position](pending)
        owner = torus.row(node[1], node[2])
        for index in reversed(carried):
            first, count = transfers[index][2:4]
            sent[index].wait_recv()
            if brought:
                rows = pl.ds(first, count)
                total[owner, rows] = (
                    total[owner, rows].astype(jnp.float32)
                    + arrived[index, :count].astype(jnp.float32)
                ).astype(total.dtype)
        for index in reversed(brought):
            sent[index] = copy(index, node)

    me = torus.row(0, 0)
    sums = {}
    for node, brought, carried in order[:2]:
        first = min(transfers[index][2] for index in carried)
        full = max(transfers[index][2] + transfers[index][3] for index in carried) - first
        part = total[me, first : first + full].astype(jnp.float32)
        for index in carried:
            lead, count = transfers[index][2:4]
            came = arrived[index, :count].astype(jnp.float32)
            if count < full:
                filler = jnp.zeros((full - count, came.shape[1]), jnp.float32)
                came = jnp.concatenate([came, filler] if lead == first else [filler, came], axis=0)
            part = part + came
        sums[node[0]] = part
    result = (self_grad + jnp.concatenate([sums[0], sums[1]], axis=0)).astype(jnp.bfloat16)
    grad_in[...] = lax.dot_general(
        row_order(result.shape[0]), result, (((0,), (0,)), ((), ())), preferred_element_type=jnp.float32
    ).astype(grad_in.dtype)
    for each in pending:
        each.wait_recv()
    rows = all_sums.shape[1] // 2
    for c in range(n_col):
        grad_self[c * rows : (c + 1) * rows] = all_sums[c, :rows]
        grad_neigh[c * rows : (c + 1) * rows] = all_sums[c, rows:]
    for each in started:
        each.wait_send()


def shards(features, grad_out, degrees, w_self, w_neigh, bias, tile_slots, tile_count, tile_masks):
    size, width = features.shape
    n_row, n_col = lax.axis_size("row"), lax.axis_size("col")
    nx, nz = 4, n_row // 4
    split = (size // 2, size // 2)
    transfers, order = torus_plan(nx, nz, split)
    copies = len(transfers)
    bf16, f32 = jnp.bfloat16, jnp.float32
    dma = pltpu.SemaphoreType.DMA
    slots, count, masks = tile_slots[0, 0], tile_count[0], tile_masks[0, 0]
    block_rows = size * n_col // TILE
    block_columns = size * n_row // TILE

    def remote(identity):
        return pltpu.CompilerParams(
            collective_id=identity, has_side_effects=True, vmem_limit_bytes=VMEM_BYTES
        )

    panel = pl.pallas_call(
        functools.partial(gather_kernel, transfers, order, nx, nz),
        name="gather_panel",
        out_shape=jax.ShapeDtypeStruct((n_row, size, width), bf16),
        in_specs=[VMEM],
        out_specs=ANY,
        scratch_shapes=[pltpu.VMEM((size, width), bf16), dma, dma((copies,)), dma((copies,))],
        compiler_params=remote(0),
    )(features)

    partial = pl.pallas_call(
        aggregate_kernel,
        name="aggregate",
        out_shape=jax.ShapeDtypeStruct((block_rows, TILE, width), bf16),
        in_specs=[SMEM, SMEM, VMEM, VMEM],
        out_specs=VMEM,
        scratch_shapes=[pltpu.VMEM((block_rows, TILE, width), f32)],
        compiler_params=pltpu.CompilerParams(vmem_limit_bytes=VMEM_BYTES),
    )(slots, count, masks, panel.reshape(block_columns, TILE, width))

    others = n_col - 1
    grad_rows = 2 * width // n_col
    layer_out, grad_preact, upward_rows, grad_sums = pl.pallas_call(
        functools.partial(middle_kernel, n_col),
        name="middle",
        out_shape=(
            jax.ShapeDtypeStruct((size, width), bf16),
            jax.ShapeDtypeStruct((size, width), bf16),
            jax.ShapeDtypeStruct((n_col, size, width), bf16),
            jax.ShapeDtypeStruct((grad_rows, width), f32),
        ),
        in_specs=[VMEM] * 7,
        out_specs=(VMEM, VMEM, ANY, VMEM),
        scratch_shapes=[
            pltpu.VMEM((others, size, width), bf16),
            pltpu.VMEM((size, width), bf16),
            pltpu.VMEM((n_col, grad_rows, width), bf16),
            pltpu.VMEM((others, grad_rows, width), bf16),
            dma,
        ]
        + [dma((others,))] * 6,
        compiler_params=remote(1),
    )(
        partial.reshape(n_col, size, width),
        features,
        grad_out,
        degrees[None, :],
        w_self,
        w_neigh,
        bias[None, :],
    )

    spread = pl.pallas_call(
        spread_kernel,
        name="spread",
        out_shape=jax.ShapeDtypeStruct((block_columns, TILE, width), bf16),
        in_specs=[SMEM, SMEM, VMEM, VMEM],
        out_specs=VMEM,
        scratch_shapes=[pltpu.VMEM((block_columns, TILE, width), f32)],
        compiler_params=pltpu.CompilerParams(vmem_limit_bytes=VMEM_BYTES),
    )(slots, count, masks, upward_rows.reshape(block_rows, TILE, width))

    grad_scale = 1.0 / math.sqrt(size * n_row * n_col)
    z_rows = grad_rows // nz
    grad_in, grad_self, grad_neigh = pl.pallas_call(
        functools.partial(scatter_kernel, transfers, order, nx, nz, n_col, grad_scale),
        name="scatter_panel",
        out_shape=(
            jax.ShapeDtypeStruct((size, width), bf16),
            jax.ShapeDtypeStruct((width, width), f32),
            jax.ShapeDtypeStruct((width, width), f32),
        ),
        in_specs=[ANY, VMEM, VMEM, VMEM],
        out_specs=(VMEM, VMEM, VMEM),
        scratch_shapes=[
            pltpu.VMEM((n_row, size, width), bf16),
            pltpu.VMEM((copies, max(split), width), bf16),
            pltpu.VMEM((nz - 1, z_rows, width), f32),
            pltpu.VMEM((nx, z_rows, width), f32),
            pltpu.VMEM((nz, z_rows, width), f32),
            pltpu.VMEM((n_col, grad_rows, width), f32),
            dma,
            dma((copies,)),
            dma((copies,)),
        ]
        + [dma((nz - 1,))] * 2
        + [dma((nx - 1,))] * 2
        + [dma((nz - 1,))] * 2
        + [dma((others,))] * 2,
        compiler_params=remote(2),
    )(
        spread.reshape(n_row, size, width),
        grad_preact,
        w_self,
        grad_sums.reshape(nz, z_rows, width),
    )
    return (layer_out, grad_in, grad_self, grad_neigh)


def solution(mesh):
    placed = (
        P(("row", "col"), None),
        P(("row", "col"), None),
        P(("row", "col")),
        P(),
        P(),
        P(),
        P("row", "col", None),
        P("row", "col"),
        P("row", "col", None, None, None),
    )
    return jax.shard_map(
        shards,
        mesh=mesh,
        in_specs=placed,
        out_specs=(P(("row", "col"), None), P(("row", "col"), None), P(), P()),
        check_vma=False,
    )
```

time: 1310 us -> 154 us (0.12)
  waiting for transfers between devices: 1030 us -> 0 us
  local copies, waits for them, and re-layouts: 174 us -> 5.57 us
  Pallas kernels: 0 us -> 144 us
  other arithmetic: 54.6 us -> 0 us
  matrix products: 19.3 us -> 0 us
  between operations: 15.8 us -> 1.32 us
    reduce_scatter x2 -> x0, waiting for transfers between devices: 715 us -> none  [the longest x1 494 us: shards(): lax.psum_scatter(partial_value.astype(jnp.bfloat16), 'col', scatter_dimen...]
    psum x1 -> x0, waiting for transfers between devices: 201 us -> none  [shards(): grad_self, grad_neigh = lax.psum((grad_self, grad_neigh), ('row', 'col'))]
    gather x174 -> x0, local copies, waits for them, and re-layouts: 167 us -> none
    pallas_call x0 -> x5, Pallas kernels: none -> 144 us  [the longest x1 49.1 us: shards(): pl.pallas_call(functools.partial(gather_kernel, transfers, order, nx, nz)...]
    all_gather x2 -> x0, waiting for transfers between devices: 108 us -> none  [the longest x1 84 us: shards(): panel = lax.all_gather(features, 'row', axis=0, tiled=True)]
    scatter-add x12 -> x0, other arithmetic: 27 us -> none  [the longest x6 19 us: spread_one_group(): return running.at[column_block - first_block].add(products)]
    dot_general x18 -> x0, matrix products: 19.3 us -> none  [the longest x6 9.64 us: aggregate_one_group(): jnp.einsum('gji,gjf->gif', tile_bits.astype(jnp.bfloat16), blocks, prefer...]
  transfers between devices with their start and end apart: 5 -> 0, of which waited for: 5 -> 0; matrix products, arithmetic and copies ran while one was open for 5% -> 0% of each run, Pallas kernels for 0% -> 0%
where the time goes in v1:
time: 154 us; the launch traced here: 151 us
  Pallas kernels  144 us (94%)
  local copies, waits for them, and re-layouts  5.57 us (4%)
    pallas_call x1, Pallas kernels, shards(): pl.pallas_call(functools.partial(gather_kernel, transfers, order, nx, nz)...  49.1 us
    pallas_call x1, Pallas kernels, shards(): pl.pallas_call(functools.partial(scatter_kernel, transfers, order, nx, nz...  49 us
    pallas_call x1, Pallas kernels, shards(): pl.pallas_call(functools.partial(middle_kernel, n_col), name='middle', ou...  31.8 us
    pallas_call x1, Pallas kernels, shards(): pl.pallas_call(spread_kernel, name='spread', out_shape=jax.ShapeDtypeStru...  7.72 us
    pallas_call x1, Pallas kernels, shards(): pl.pallas_call(aggregate_kernel, name='aggregate', out_shape=jax.ShapeDty...  6.86 us
    unnamed x6, local copies, waits for them, and re-layouts  5.57 us

profile of v1, /device:TPU:8, one launch (start us, length us, event | category | flops | bytes accessed | tf_op | source)
XLA Modules:
  0.0 151.4 jit_solution(4338764041162013377)
XLA Ops:
  1.3 49.1 %gather_panel.1 = bf16[32,256,256]{2,1,0:T(8,128)(2,1)} custom-call(bf16[256,256]{1,0:T(8,128)(2,1)} %features.3), custom_call_target="tpu_custom_call" | custom-call | tf_op jit(solution)/shard_map/gather_panel/pallas_call | solution.py:435
  50.4 6.9 %aggregate.1 = bf16[16,128,256]{2,1,0:T(8,128)(2,1)} custom-call(s32[176]{0:T(256)} %bitcast.19, s32[1]{0:T(128)} %bitcast.10.count, s32[176,16,128]{2,1,0:T(8,128)} %bitcast.14, bf16[64,128,256]{2,1,0:T(8,128)(2,1)} %bitcast.13), custom_call_target="tpu_custom_call" | custom-call | tf_op jit(solution)/shard_map/aggregate/pallas_call | solution.py:445
  57.2 31.8 %middle.1 = (bf16[256,256]{1,0:T(8,128)(2,1)}, bf16[256,256]{1,0:T(8,128)(2,1)}, bf16[8,256,256]{2,1,0:T(8,128)(2,1)}, f32[64,256]{1,0:T(8,128)}) custom-call(bf16[8,256,256]{2,1,0:T(8,128)(2,1)} %bitcast.16, bf16[256,256]{1,0:T(8,128)(2,1)} %features.3, bf16[256,256]{1,0:T(8,128)(2,1)} %grad_out.1, s32[1,256]{1,0:T(1,128)} %bitcast.21, ...), custom_call_target="tpu_custom_call" | custom-call | tf_op jit(solution)/shard_map/middle/pallas_call | solution.py:457
  89.0 0.0 copy-start
  89.0 7.7 %spread.1 = bf16[64,128,256]{2,1,0:T(8,128)(2,1)} custom-call(s32[176]{0:T(256)} %bitcast.20, s32[1]{0:T(128)} %bitcast.11.count, s32[176,16,128]{2,1,0:T(8,128)} %bitcast.15, bf16[16,128,256]{2,1,0:T(8,128)(2,1)} %bitcast.17), custom_call_target="tpu_custom_call" | custom-call | tf_op jit(solution)/shard_map/spread/pallas_call | solution.py:487
  96.7 49.0 %scatter_panel.1 = (bf16[256,256]{1,0:T(8,128)(2,1)}, f32[256,256]{1,0:T(8,128)}, f32[256,256]{1,0:T(8,128)}) custom-call(bf16[32,256,256]{2,1,0:T(8,128)(2,1)} %bitcast.12, bf16[256,256]{1,0:T(8,128)(2,1)} %get-tuple-element.13.grad_preact, bf16[256,256]{1,0:T(8,128)(2,1)} %w_self.3, f32[8,8,256]{2,1,0:T(8,128)} %bitcast.18), custom_call_target="tpu_custom_call" | custom-call | tf_op jit(solution)/shard_map/scatter_panel/pallas_call | solution.py:499
  145.8 0.0 copy-done
  145.8 0.7 copy.18
  146.5 1.6 %copy.19 = bf16[256,256]{1,0:T(8,128)(2,1)} copy(bf16[256,256]{1,0:T(8,128)(2,1)} %get-tuple-element.23) | data formatting | bytes 262144
  148.0 1.7 %copy.20 = f32[256,256]{1,0:T(8,128)} copy(f32[256,256]{1,0:T(8,128)} %get-tuple-element.24) | data formatting | bytes 524288
  149.7 1.7 %copy.21 = f32[256,256]{1,0:T(8,128)} copy(f32[256,256]{1,0:T(8,128)} %get-tuple-element.25) | data formatting | bytes 524288
Async XLA Ops:
  89.0 56.8 %copy-start = (bf16[256,256]{1,0:T(8,128)(2,1)S(1)}, bf16[256,256]{1,0:T(8,128)(2,1)}, u32[]{:S(2)}) copy-start(bf16[256,256]{1,0:T(8,128)(2,1)} %get-tuple-element.22) | copy-start | bytes 393220

commit v2 on v1

v2 whole, which is shorter than its diff:
```python
import functools
import heapq
import math

import jax
import jax.numpy as jnp
from jax import lax
from jax.experimental import pallas as pl
from jax.experimental.pallas import tpu as pltpu
from jax.sharding import PartitionSpec as P

MESH = pl.DeviceIdType.MESH
SMEM = pl.BlockSpec(memory_space=pltpu.SMEM)
VMEM = pl.BlockSpec(memory_space=pltpu.VMEM)
ANY = pl.BlockSpec(memory_space=pl.ANY)
TILE = 128
UNROLL = 16


def torus_plan(nx, nz, split, latency=1.0, rate=0.01):
    size = {"x": nx, "z": nz}
    transfers, order = [], []
    free, heap = {}, []

    def wrap(d, n):
        d %= n
        return d - n if d > n // 2 else d

    def send(now, node, axis, sign, first, count):
        offset = {"x": node[1], "z": node[2]}
        offset[axis] = wrap(offset[axis] - sign, size[axis])
        index = len(transfers)
        transfers.append((axis, sign, first, count, (node[0], offset["x"], offset["z"])))
        start = max(now, free.get((axis, sign), 0.0))
        free[axis, sign] = start + count * rate
        heapq.heappush(heap, (free[axis, sign] + latency, index))
        entries[node][1].append(index)

    def forward(now, node, phases="pq"):
        part = node[0]
        (p, q), begin, full = split[part]
        offset = {"x": node[1], "z": node[2]}
        dp, dq = offset[p], offset[q]
        half_p, half_q = size[p] // 2, size[q] // 2
        lower = (full // 2 + 15) // 16 * 16
        for sign in (1, -1) if "p" in phases else ():
            if dq == 0 and (dp == 0 or -dp * sign > 0) and dp != half_p:
                if abs(dp) + 1 < half_p:
                    send(now, node, p, sign, begin, full)
                elif sign == 1:
                    send(now, node, p, sign, begin, lower)
                else:
                    send(now, node, p, sign, begin + lower, full - lower)
        for sign in (1, -1) if "q" in phases else ():
            if (dq == 0 or -dq * sign > 0) and dq != half_q:
                if abs(dq) + 1 < half_q or (0 <= dp < half_p) == (sign == 1):
                    send(now, node, q, sign, begin, full)

    got = {}
    entries = {(part, 0, 0): ([], []) for part in range(len(split))}
    roots = []
    for phases in "pq":
        for part in range(len(split)):
            forward(0.0, (part, 0, 0), phases)
            roots.append(((part, 0, 0), [], entries[part, 0, 0][1]))
            entries[part, 0, 0] = ([], [])
    while heap:
        now, index = heapq.heappop(heap)
        count, node = transfers[index][3:]
        entries.setdefault(node, ([], []))[0].append(index)
        got[node] = got.get(node, 0) + count
        if got[node] == split[node[0]][2]:
            order.append(node)
            forward(now, node)
    return transfers, roots + [(node, *entries[node]) for node in order]


class Torus:
    def __init__(self, nx, nz):
        self.nx, self.nz = nx, nz
        row = lax.axis_index("row")
        self.x, self.z = lax.rem(row, nx), lax.div(row, nx)

    def row(self, dx, dz):
        x = lax.rem(self.x + (dx + self.nx), self.nx)
        z = lax.rem(self.z + (dz + self.nz), self.nz)
        return z * self.nx + x

    def neighbour(self, axis, sign):
        return {"row": self.row(sign, 0) if axis == "x" else self.row(0, sign)}


def greet(barrier, peers):
    for peer in peers:
        pl.semaphore_signal(barrier, inc=1, device_id=peer, device_id_type=MESH)


def row_order(size):
    place = lax.broadcasted_iota(jnp.int32, (size, size), 0)
    node = lax.broadcasted_iota(jnp.int32, (size, size), 1)
    within = place & (TILE - 1)
    source = (place - within) + ((within & 15) << 3) + (within >> 4)
    return jnp.where(source == node, 1.0, 0.0).astype(jnp.bfloat16)


def gather_kernel(transfers, order, nx, nz, features, panel, own, local_sem, send_sem, recv_sem):
    torus = Torus(nx, nz)
    me = torus.row(0, 0)
    barrier = pltpu.get_barrier_semaphore()
    around = [torus.neighbour(axis, sign) for axis in "xz" for sign in (1, -1)]
    greet(barrier, around)
    own[...] = jnp.dot(
        row_order(own.shape[0]), features[...], preferred_element_type=jnp.float32
    ).astype(own.dtype)
    pl.semaphore_wait(barrier, len(around))

    def copy(index, node, source):
        axis, sign, first, count, _ = transfers[index]
        origin = torus.row(node[1], node[2])
        rows = pl.ds(first, count)
        return pltpu.make_async_remote_copy(
            src_ref=own.at[rows] if source else panel.at[origin, rows],
            dst_ref=panel.at[origin, rows],
            send_sem=send_sem.at[index],
            recv_sem=recv_sem.at[index],
            device_id=torus.neighbour(axis, sign),
            device_id_type=MESH,
        )

    started = []
    for node, brought, carried in order:
        for index in brought:
            copy(index, node, False).wait_recv()
        for index in carried:
            started.append(copy(index, node, not brought))
            started[-1].start()
    keep = pltpu.make_async_copy(own, panel.at[me], local_sem)
    keep.start()
    for each in started:
        each.wait_send()
    keep.wait()


def unpack(words):
    return jnp.concatenate(
        [((words >> bit) & 1).astype(jnp.float32).astype(jnp.bfloat16) for bit in range(8)], axis=0
    )


def each_tile(slots, live, masks, block_rows, step):
    last = masks.shape[0] - 1

    def group(index, _):
        for u in range(UNROLL):
            tile = index * UNROLL + u
            held = jnp.minimum(tile, last)
            slot = slots[held]
            words = jnp.where(tile < live, masks[held], 0)
            step(lax.rem(slot, block_rows), lax.div(slot, block_rows), unpack(words))
        return 0

    lax.fori_loop(0, lax.div(live + (UNROLL - 1), UNROLL), group, 0)


def set_zero(total):
    def one(i, _):
        total[i] = jnp.zeros(total.shape[1:], total.dtype)
        return 0

    lax.fori_loop(0, total.shape[0], one, 0)


def round_to(out, total):
    def one(i, _):
        out[i] = total[i].astype(out.dtype)
        return 0

    lax.fori_loop(0, total.shape[0], one, 0)


def aggregate_kernel(slots, count, masks, panel, out, total):
    set_zero(total)

    def step(row_block, column_block, bits):
        total[row_block] += lax.dot_general(
            bits, panel[column_block], (((0,), (0,)), ((), ())), preferred_element_type=jnp.float32
        )

    each_tile(slots, count[0], masks, out.shape[0], step)
    round_to(out, total)


def spread_kernel(slots, count, masks, upward, layer_in, out, layer_out, total, layer_sem):
    hand_on = pltpu.make_async_copy(layer_in, layer_out, layer_sem)
    hand_on.start()
    set_zero(total)

    def step(row_block, column_block, bits):
        total[column_block] += jnp.dot(bits, upward[row_block], preferred_element_type=jnp.float32)

    each_tile(slots, count[0], masks, upward.shape[0], step)
    round_to(out, total)
    hand_on.wait()


def middle_kernel(
    partial, features, grad_out, degrees, w_self, w_neigh, bias,
    layer_out, mean_rows, grad_preact, upward_rows,
    own_part, scale, from_sibling, joined, arrived, own_sum, upward,
    keep_sem, sibling_send, sibling_recv, y_send, y_recv, up_send, up_recv, pass_send, pass_recv,
):
    col = lax.axis_index("col")
    y, core = lax.div(col, 2), lax.rem(col, 2)
    ny = partial.shape[0] // 2
    halves, rows = partial.shape[1:3]
    place = [lax.rem(y + k, ny) for k in range(ny)]
    far_first = sorted(range(1, ny), key=lambda k: -min(k, ny - k))
    sibling = {"col": 2 * y + 1 - core}
    along_y = [{"col": 2 * place[k] + core} for k in range(ny)]
    barrier = pltpu.get_barrier_semaphore()
    greet(barrier, [sibling, *along_y[1:]])
    size, width = features.shape
    scale[...] = jnp.broadcast_to(degrees[...].astype(jnp.float32), (width, size)).T
    own_part[...] = bias[...] + jnp.dot(
        features[...], w_self[...], preferred_element_type=jnp.float32
    )
    pl.semaphore_wait(barrier, ny)

    started = []

    def start(source, target, sends, recvs, k, peer):
        copy = pltpu.make_async_remote_copy(
            src_ref=source,
            dst_ref=target,
            send_sem=sends.at[k],
            recv_sem=recvs.at[k],
            device_id=peer,
            device_id_type=MESH,
        )
        copy.start()
        started.append(copy)
        return copy

    pieces = [(half, k) for half in range(halves) for k in (*far_first, 0)]
    shared = {}
    for half, k in pieces:
        shared[half, k] = start(
            partial.at[2 * place[k] + 1 - core, half], from_sibling.at[k, half],
            sibling_send, sibling_recv, half * ny + k, sibling,
        )
    exchanged = {}
    for half, k in pieces:
        shared[half, k].wait_recv()
        both = partial[2 * place[k] + core, half].astype(jnp.float32)
        both = both + from_sibling[k, half].astype(jnp.float32)
        if k == 0:
            own_sum[half] = both
        else:
            joined[k - 1, half] = both.astype(joined.dtype)
            exchanged[half, k] = start(
                joined.at[k - 1, half], arrived.at[k - 1, half],
                y_send, y_recv, half * (ny - 1) + k - 1, along_y[k],
            )
    gathered, passed, kept = {}, [], []
    for half in range(halves):
        summed = own_sum[half]
        for k in far_first:
            exchanged[half, k].wait_recv()
            summed = summed + arrived[k - 1, half].astype(jnp.float32)
        here = slice(half * rows, (half + 1) * rows)
        mean = (summed / scale[here]).astype(mean_rows.dtype)
        preact = own_part[here] + jnp.dot(mean, w_neigh[...], preferred_element_type=jnp.float32)
        sigmoid_values = jax.nn.sigmoid(preact)
        gradient = (
            grad_out[here].astype(jnp.float32) * sigmoid_values * (1.0 + preact * (1.0 - sigmoid_values))
        ).astype(grad_preact.dtype)
        sent_up = lax.dot_general(
            gradient, w_neigh[...], (((1,), (1,)), ((), ())), preferred_element_type=jnp.float32
        )
        upward[half] = (sent_up / scale[here]).astype(upward.dtype)
        target = upward_rows.at[col, half]
        for k in far_first:
            gathered[half, k] = start(
                upward.at[half], target, up_send, up_recv, half * (ny - 1) + k - 1, along_y[k]
            )
        passed.append(start(upward.at[half], target, pass_send, pass_recv, half * ny, sibling))
        kept.append(pltpu.make_async_copy(upward.at[half], target, keep_sem.at[half]))
        kept[-1].start()
        layer_out[here] = (preact * sigmoid_values).astype(layer_out.dtype)
        mean_rows[here] = mean
        grad_preact[here] = gradient
    for half in range(halves):
        for k in reversed(far_first):
            gathered[half, k].wait_recv()
            held = upward_rows.at[2 * lax.rem(y + ny - k, ny) + core, half]
            passed.append(start(held, held, pass_send, pass_recv, half * ny + k, sibling))
    for each in passed:
        each.wait_recv()
    for each in started:
        each.wait_send()
    for each in kept:
        each.wait()


def scatter_kernel(
    transfers, order, n_parts, nx, nz, n_col, grad_scale, partial, features, mean_rows, grad_preact, w_self,
    moved_in, weight_sums,
    total, arrived, parts, col_arrived, col_sums, z_arrived, x_sums, z_sums, all_sums,
    load_sem, send_sem, recv_sem, c_send, c_recv, z_send, z_recv, x_send, x_recv, zz_send, zz_recv, cc_send, cc_recv,
):
    torus = Torus(nx, nz)
    col = lax.axis_index("col")
    load = pltpu.make_async_copy(partial, total, load_sem)
    load.start()
    barrier = pltpu.get_barrier_semaphore()
    along_z = [{"row": torus.row(0, k)} for k in range(1, nz)]
    along_x = [{"row": torus.row(k, 0)} for k in range(1, nx)]
    cols = [lax.rem(col + k, n_col) for k in range(n_col)]
    along_col = [{"col": c} for c in cols[1:]]
    greet(barrier, along_z + along_x + along_col)
    moved = jnp.dot(
        row_order(grad_preact.shape[0]), grad_preact[...], preferred_element_type=jnp.float32
    ).astype(jnp.bfloat16)
    self_grad = lax.dot_general(
        moved, w_self[...], (((1,), (1,)), ((), ())), preferred_element_type=jnp.float32
    )
    rows = w_self.shape[0] // n_col
    for half, source in enumerate((features, mean_rows)):
        product = lax.dot_general(
            source[...], grad_preact[...], (((0,), (0,)), ((), ())), preferred_element_type=jnp.float32
        ).astype(parts.dtype)
        for c in range(n_col):
            parts[c, half * rows : (half + 1) * rows] = product[c * rows : (c + 1) * rows]
    pl.semaphore_wait(barrier, len(along_z) + len(along_x) + len(along_col))

    started = []

    def start(source, target, sends, recvs, k, peer):
        started.append(
            pltpu.make_async_remote_copy(
                src_ref=source,
                dst_ref=target,
                send_sem=sends.at[k],
                recv_sem=recvs.at[k],
                device_id=peer,
                device_id_type=MESH,
            )
        )
        started[-1].start()
        return started[-1]

    def reduce_along_col():
        return [
            start(parts.at[cols[k]], col_arrived.at[k - 1], c_send, c_recv, k - 1, peer)
            for k, peer in enumerate(along_col, 1)
        ]

    def reduce_along_z(before):
        for each in before:
            each.wait_recv()
        part = parts[col].astype(jnp.float32)
        for k in range(n_col - 1):
            part = part + col_arrived[k].astype(jnp.float32)
        col_sums[...] = part.reshape(col_sums.shape)
        return [
            start(col_sums.at[lax.rem(torus.z + k, nz)], z_arrived.at[k - 1], z_send, z_recv, k - 1, peer)
            for k, peer in enumerate(along_z, 1)
        ]

    def reduce_along_x(before):
        for each in before:
            each.wait_recv()
        part = col_sums[torus.z]
        for k in range(nz - 1):
            part = part + z_arrived[k]
        x_sums[torus.x] = part
        return [
            start(x_sums.at[torus.x], x_sums.at[torus.x], x_send, x_recv, k, peer)
            for k, peer in enumerate(along_x)
        ]

    def gather_along_z(before):
        for each in before:
            each.wait_recv()
        part = x_sums[0]
        for k in range(1, nx):
            part = part + x_sums[k]
        z_sums[torus.z] = part * grad_scale
        return [
            start(z_sums.at[torus.z], z_sums.at[torus.z], zz_send, zz_recv, k, peer)
            for k, peer in enumerate(along_z)
        ]

    def gather_along_col(before):
        for each in before:
            each.wait_recv()
        all_sums[col] = z_sums[...].reshape(all_sums.shape[1:])
        return [
            start(all_sums.at[col], all_sums.at[col], cc_send, cc_recv, k, peer)
            for k, peer in enumerate(along_col)
        ]

    def copy(index, node):
        axis, sign, first, count, _ = transfers[index]
        return start(
            total.at[torus.row(node[1], node[2]), pl.ds(first, count)],
            arrived.at[index, pl.ds(0, count)],
            send_sem,
            recv_sem,
            index,
            torus.neighbour(axis, -sign),
        )

    sent = {}
    pending = reduce_along_col()
    steps = (reduce_along_z, reduce_along_x, gather_along_z, gather_along_col)
    stages = {len(order) * (k + 2) // 7: step for k, step in enumerate(steps)}
    load.wait()
    for position, (node, brought, carried) in enumerate(reversed(order)):
        if position in stages:
            pending = stages[position](pending)
        owner = torus.row(node[1], node[2])
        for index in reversed(carried):
            first, count = transfers[index][2:4]
            sent[index].wait_recv()
            if brought:
                rows = pl.ds(first, count)
                total[owner, rows] = (
                    total[owner, rows].astype(jnp.float32)
                    + arrived[index, :count].astype(jnp.float32)
                ).astype(total.dtype)
        for index in reversed(brought):
            sent[index] = copy(index, node)

    me = torus.row(0, 0)
    sums = []
    for (node, _, first_carried), (_, _, carried) in zip(order[:n_parts], order[n_parts:]):
        carried = first_carried + carried
        first = min(transfers[index][2] for index in carried)
        full = max(transfers[index][2] + transfers[index][3] for index in carried) - first
        part = total[me, first : first + full].astype(jnp.float32)
        for index in carried:
            lead, count = transfers[index][2:4]
            came = arrived[index, :count].astype(jnp.float32)
            if count < full:
                filler = jnp.zeros((full - count, came.shape[1]), jnp.float32)
                came = jnp.concatenate([came, filler] if lead == first else [filler, came], axis=0)
            part = part + came
        sums.append((first, part))
    neighbour_sum = jnp.concatenate([part for _, part in sorted(sums, key=lambda pair: pair[0])], axis=0)
    moved_in[...] = (self_grad + neighbour_sum).astype(moved_in.dtype)
    for each in pending:
        each.wait_recv()
    weight_sums[...] = all_sums[...]
    for each in started:
        each.wait_send()


def finish_kernel(moved_in, weight_sums, grad_in, grad_self, grad_neigh):
    grad_in[...] = lax.dot_general(
        row_order(moved_in.shape[0]), moved_in[...], (((0,), (0,)), ((), ())), preferred_element_type=jnp.float32
    ).astype(grad_in.dtype)
    rows = weight_sums.shape[1] // 2
    for c in range(weight_sums.shape[0]):
        grad_self[c * rows : (c + 1) * rows] = weight_sums[c, :rows]
        grad_neigh[c * rows : (c + 1) * rows] = weight_sums[c, rows:]


def shards(features, grad_out, degrees, w_self, w_neigh, bias, tile_slots, tile_count, tile_masks):
    size, width = features.shape
    n_row, n_col = lax.axis_size("row"), lax.axis_size("col")
    nx, nz = 4, n_row // 4
    split = [("xz", 0, 48), ("xz", 48, 48), ("zx", 96, 80), ("zx", 176, 80)]
    transfers, order = torus_plan(nx, nz, split)
    copies = len(transfers)
    bf16, f32 = jnp.bfloat16, jnp.float32
    dma = pltpu.SemaphoreType.DMA
    slots, count, masks = tile_slots[0, 0], tile_count[0], tile_masks[0, 0]
    block_rows = size * n_col // TILE
    block_columns = size * n_row // TILE
    halves = size // TILE
    ny = n_col // 2

    def array(dtype, *shape):
        return jax.ShapeDtypeStruct(shape, dtype)

    def local(mib):
        return pltpu.CompilerParams(vmem_limit_bytes=mib << 20)

    def remote(identity, mib):
        return pltpu.CompilerParams(
            collective_id=identity, has_side_effects=True, vmem_limit_bytes=mib << 20
        )

    panel = pl.pallas_call(
        functools.partial(gather_kernel, transfers, order, nx, nz),
        name="gather_panel",
        out_shape=array(bf16, n_row, size, width),
        in_specs=[VMEM],
        out_specs=ANY,
        scratch_shapes=[pltpu.VMEM((size, width), bf16), dma, dma((copies,)), dma((copies,))],
        compiler_params=remote(0, 4),
    )(features)

    partial = pl.pallas_call(
        aggregate_kernel,
        name="aggregate",
        out_shape=array(bf16, block_rows, TILE, width),
        in_specs=[SMEM, SMEM, VMEM, VMEM],
        out_specs=VMEM,
        scratch_shapes=[pltpu.VMEM((block_rows, TILE, width), f32)],
        compiler_params=local(16),
    )(slots, count, masks, panel.reshape(block_columns, TILE, width))

    layer_in, mean_rows, grad_preact, upward_rows = pl.pallas_call(
        middle_kernel,
        name="middle",
        out_shape=(
            array(bf16, size, width),
            array(bf16, size, width),
            array(bf16, size, width),
            array(bf16, n_col, halves, TILE, width),
        ),
        in_specs=[VMEM] * 7,
        out_specs=(VMEM, VMEM, VMEM, ANY),
        scratch_shapes=[
            pltpu.VMEM((size, width), f32),
            pltpu.VMEM((size, width), f32),
            pltpu.VMEM((ny, halves, TILE, width), bf16),
            pltpu.VMEM((ny - 1, halves, TILE, width), bf16),
            pltpu.VMEM((ny - 1, halves, TILE, width), bf16),
            pltpu.VMEM((halves, TILE, width), f32),
            pltpu.VMEM((halves, TILE, width), bf16),
            dma((halves,)),
        ]
        + [dma((ny * halves,))] * 2
        + [dma(((ny - 1) * halves,))] * 4
        + [dma((ny * halves,))] * 2,
        compiler_params=remote(1, 16),
    )(
        partial.reshape(n_col, halves, TILE, width),
        features,
        grad_out,
        degrees[None, :],
        w_self,
        w_neigh,
        bias[None, :],
    )

    spread, layer_out = pl.pallas_call(
        spread_kernel,
        name="spread",
        out_shape=(array(bf16, block_columns, TILE, width), array(bf16, size, width)),
        in_specs=[SMEM, SMEM, VMEM, VMEM, ANY],
        out_specs=(VMEM, ANY),
        scratch_shapes=[pltpu.VMEM((block_columns, TILE, width), f32), dma],
        compiler_params=local(24),
    )(slots, count, masks, upward_rows.reshape(block_rows, TILE, width), layer_in)

    grad_scale = 1.0 / math.sqrt(size * n_row * n_col)
    grad_rows = 2 * width // n_col
    z_rows = grad_rows // nz
    others = n_col - 1
    moved_in, weight_sums = pl.pallas_call(
        functools.partial(scatter_kernel, transfers, order, len(split), nx, nz, n_col, grad_scale),
        name="scatter_panel",
        out_shape=(array(bf16, size, width), array(f32, n_col, grad_rows, width)),
        in_specs=[ANY, VMEM, VMEM, VMEM, VMEM],
        out_specs=(VMEM, VMEM),
        scratch_shapes=[
            pltpu.VMEM((n_row, size, width), bf16),
            pltpu.VMEM((copies, max(part[2] for part in split), width), bf16),
            pltpu.VMEM((n_col, grad_rows, width), bf16),
            pltpu.VMEM((others, grad_rows, width), bf16),
            pltpu.VMEM((nz, z_rows, width), f32),
            pltpu.VMEM((nz - 1, z_rows, width), f32),
            pltpu.VMEM((nx, z_rows, width), f32),
            pltpu.VMEM((nz, z_rows, width), f32),
            pltpu.VMEM((n_col, grad_rows, width), f32),
            dma,
            dma((copies,)),
            dma((copies,)),
        ]
        + [dma((others,))] * 2
        + [dma((nz - 1,))] * 2
        + [dma((nx - 1,))] * 2
        + [dma((nz - 1,))] * 2
        + [dma((others,))] * 2,
        compiler_params=remote(2, 24),
    )(spread.reshape(n_row, size, width), features, mean_rows, grad_preact, w_self)

    grad_in, grad_self, grad_neigh = pl.pallas_call(
        finish_kernel,
        name="finish",
        out_shape=(array(bf16, size, width), array(f32, width, width), array(f32, width, width)),
        in_specs=[VMEM, VMEM],
        out_specs=(VMEM, VMEM, VMEM),
        compiler_params=local(8),
    )(moved_in, weight_sums)
    return (layer_out, grad_in, grad_self, grad_neigh)


def solution(mesh):
    placed = (
        P(("row", "col"), None),
        P(("row", "col"), None),
        P(("row", "col")),
        P(),
        P(),
        P(),
        P("row", "col", None),
        P("row", "col"),
        P("row", "col", None, None, None),
    )
    return jax.shard_map(
        shards,
        mesh=mesh,
        in_specs=placed,
        out_specs=(P(("row", "col"), None), P(("row", "col"), None), P(), P()),
        check_vma=False,
    )
```

time: 154 us -> 112 us (0.73); the launches traced: 151 us -> 111 us
  Pallas kernels: 144 us -> 109 us
  local copies, waits for them, and re-layouts: 5.57 us -> 0.95 us
    pallas_call x4 -> x5, Pallas kernels: 95.4 us -> 72.5 us  [the longest x1 44.1 us: shards(): pl.pallas_call(functools.partial(scatter_kernel, transfers, order, len(sp...]
    pallas_call x1, Pallas kernels: 49.1 us -> 36.2 us  [shards(): pl.pallas_call(functools.partial(gather_kernel, transfers, order, nx, nz)...]
    unnamed x6 -> x18, local copies, waits for them, and re-layouts: 5.57 us -> 0.95 us
where the time goes in v2:
time: 112 us; the launch traced here: 111 us
  Pallas kernels  109 us (97%)
  between operations  1.56 us (1%)
    pallas_call x1, Pallas kernels, shards(): pl.pallas_call(functools.partial(scatter_kernel, transfers, order, len(sp...  44.1 us
    pallas_call x1, Pallas kernels, shards(): pl.pallas_call(functools.partial(gather_kernel, transfers, order, nx, nz)...  36.2 us
    pallas_call x1, Pallas kernels, shards(): pl.pallas_call(middle_kernel, name='middle', out_shape=(array(bf16, size,...  21.8 us
    pallas_call x1, Pallas kernels, shards(): pl.pallas_call(spread_kernel, name='spread', out_shape=(array(bf16, block...  3.28 us
    pallas_call x1, Pallas kernels, shards(): pl.pallas_call(aggregate_kernel, name='aggregate', out_shape=array(bf16,...  2.36 us

profile of v2, /device:TPU:8, one launch (start us, length us, event | category | flops | bytes accessed | tf_op | source)
XLA Modules:
  0.0 111.3 jit_solution(13121140972770743253)
XLA Ops:
  0.6 0.0 copy-start
  1.4 0.0 copy-start.1
  1.4 0.9 copy-done.1
  2.3 0.0 copy-start.6
  2.3 36.2 %gather_panel.1 = bf16[32,256,256]{2,1,0:T(8,128)(2,1)S(1)} custom-call(bf16[256,256]{1,0:T(8,128)(2,1)S(1)} %copy-done.1), custom_call_target="tpu_custom_call" | custom-call | tf_op jit(solution)/shard_map/gather_panel/pallas_call | solution.py:495
  38.6 0.0 copy-start.2
  38.6 0.0 copy-start.3
  38.6 0.0 copy-start.4
  38.6 0.0 copy-start.5
  38.6 0.0 copy-start.7
  38.6 0.0 copy-start.8
  38.6 0.0 copy-done
  38.6 0.0 copy-done.6
  38.7 2.4 %aggregate.1 = bf16[16,128,256]{2,1,0:T(8,128)(2,1)S(1)} custom-call(s32[176]{0:T(256)S(1)} %bitcast.17, s32[1]{0:T(128)} %bitcast.9.count, s32[176,16,128]{2,1,0:T(8,128)S(1)} %bitcast.12, bf16[64,128,256]{2,1,0:T(8,128)(2,1)S(1)} %bitcast.11), custom_call_target="tpu_custom_call" | custom-call | tf_op jit(solution)/shard_map/aggregate/pallas_call | solution.py:505
  41.0 0.0 copy-done.2
  41.0 0.0 copy-done.3
  41.0 0.0 copy-done.4
  41.0 0.0 copy-done.5
  41.1 0.0 copy-done.7
  41.1 0.0 copy-done.8
  41.1 21.8 %middle.1 = (bf16[256,256]{1,0:T(8,128)(2,1)S(1)}, bf16[256,256]{1,0:T(8,128)(2,1)S(1)}, bf16[256,256]{1,0:T(8,128)(2,1)S(1)}, bf16[8,2,128,256]{3,2,1,0:T(8,128)(2,1)S(1)}) custom-call(bf16[8,2,128,256]{3,2,1,0:T(8,128)(2,1)S(1)} %bitcast.15, bf16[256,256]{1,0:T(8,128)(2,1)S(1)} %copy-done.2, bf16[256,256]{1,0:T(8,128)(2,1)S(1)} %copy-done.4, ...), custom_call_target="tpu_custom_call" | custom-call | tf_op jit(solution)/shard_map/middle/pallas_call | solution.py:515
  62.9 3.3 %spread.1 = (bf16[64,128,256]{2,1,0:T(8,128)(2,1)S(1)}, bf16[256,256]{1,0:T(8,128)(2,1)}) custom-call(s32[176]{0:T(256)S(1)} %bitcast.18, s32[1]{0:T(128)} %bitcast.10.count, s32[176,16,128]{2,1,0:T(8,128)S(1)} %bitcast.13, bf16[16,128,256]{2,1,0:T(8,128)(2,1)S(1)} %bitcast.16, bf16[256,256]{1,0:T(8,128)(2,1)S(1)} %get-tuple-element.16.layer_in), custom_call_target="tpu_custom_call" | custom-call | tf_op jit(solution)/shard_map/spread/pallas_call | solution.py:550
  66.1 44.1 %scatter_panel.1 = (bf16[256,256]{1,0:T(8,128)(2,1)S(1)}, f32[8,64,256]{2,1,0:T(8,128)S(1)}) custom-call(bf16[32,256,256]{2,1,0:T(8,128)(2,1)S(1)} %bitcast.14, bf16[256,256]{1,0:T(8,128)(2,1)S(1)} %copy-done.2, bf16[256,256]{1,0:T(8,128)(2,1)S(1)} %get-tuple-element.19.mean_rows, bf16[256,256]{1,0:T(8,128)(2,1)S(1)} %get-tuple-element.20.grad_preact, ...), custom_call_target="tpu_custom_call" | custom-call | tf_op jit(solution)/shard_map/scatter_panel/pallas_call | solution.py:564
  110.3 1.0 finish.1
Async XLA Ops:
  0.6 38.0 %copy-start = (s32[1,1,176,16,128]{4,3,2,1,0:T(8,128)S(1)}, s32[1,1,176,16,128]{4,3,2,1,0:T(8,128)}, u32[]{:S(2)}) copy-start(s32[1,1,176,16,128]{4,3,2,1,0:T(8,128)} %param.17) | copy-start | bytes 4325380
  1.4 0.9 copy-start.1
  2.3 36.3 %copy-start.6 = (s32[1,1,176]{2,1,0:T(1,128)S(1)}, s32[1,1,176]{2,1,0:T(1,128)}, u32[]{:S(2)}) copy-start(s32[1,1,176]{2,1,0:T(1,128)} %param.15) | copy-start | bytes 2116
  38.6 2.5 %copy-start.2 = (bf16[256,256]{1,0:T(8,128)(2,1)S(1)}, bf16[256,256]{1,0:T(8,128)(2,1)}, u32[]{:S(2)}) copy-start(bf16[256,256]{1,0:T(8,128)(2,1)} %features.5) | copy-start | bytes 393220
  38.6 2.5 %copy-start.3 = (bf16[256,256]{1,0:T(8,128)(2,1)S(1)}, bf16[256,256]{1,0:T(8,128)(2,1)}, u32[]{:S(2)}) copy-start(bf16[256,256]{1,0:T(8,128)(2,1)} %w_self.3) | copy-start | bytes 393220
  38.6 2.5 %copy-start.4 = (bf16[256,256]{1,0:T(8,128)(2,1)S(1)}, bf16[256,256]{1,0:T(8,128)(2,1)}, u32[]{:S(2)}) copy-start(bf16[256,256]{1,0:T(8,128)(2,1)} %grad_out.1) | copy-start | bytes 393220
  38.6 2.5 %copy-start.5 = (bf16[256,256]{1,0:T(8,128)(2,1)S(1)}, bf16[256,256]{1,0:T(8,128)(2,1)}, u32[]{:S(2)}) copy-start(bf16[256,256]{1,0:T(8,128)(2,1)} %w_neigh.1) | copy-start | bytes 393220
  38.6 2.5 %copy-start.7 = (s32[256]{0:T(256)S(1)}, s32[256]{0:T(256)}, u32[]{:S(2)}) copy-start(s32[256]{0:T(256)} %param.11) | copy-start | bytes 3076
  38.6 2.5 %copy-start.8 = (f32[256]{0:T(256)S(1)}, f32[256]{0:T(256)}, u32[]{:S(2)}) copy-start(f32[256]{0:T(256)} %param.14) | copy-start | bytes 3076

commit v3 on v2

--- a/solution.py
+++ b/solution.py
@@ -15,9 +15,10 @@
 ANY = pl.BlockSpec(memory_space=pl.ANY)
 TILE = 128
 UNROLL = 16
-
-
-def torus_plan(nx, nz, split, latency=1.0, rate=0.01):
+STAGES = (0, 4, 9, 30, 48, 68)
+
+
+def torus_plan(nx, nz, split, latency=3.0, rate=0.0085):
     size = {"x": nx, "z": nz}
     transfers, order = [], []
     free, heap = {}, []
@@ -127,6 +128,8 @@
             device_id_type=MESH,
         )
 
+    keep = pltpu.make_async_copy(own, panel.at[me], local_sem)
+    keep.start()
     started = []
     for node, brought, carried in order:
         for index in brought:
@@ -134,8 +137,6 @@
         for index in carried:
             started.append(copy(index, node, not brought))
             started[-1].start()
-    keep = pltpu.make_async_copy(own, panel.at[me], local_sem)
-    keep.start()
     for each in started:
         each.wait_send()
     keep.wait()
@@ -205,9 +206,9 @@
 
 def middle_kernel(
     partial, features, grad_out, degrees, w_self, w_neigh, bias,
-    layer_out, mean_rows, grad_preact, upward_rows,
-    own_part, scale, from_sibling, joined, arrived, own_sum, upward,
-    keep_sem, sibling_send, sibling_recv, y_send, y_recv, up_send, up_recv, pass_send, pass_recv,
+    layer_out, grad_preact, upward_rows, weight_sums,
+    own_part, scale, from_sibling, joined, arrived, own_sum, upward, mean_rows, parts, parts_arrived,
+    keep_sem, sibling_send, sibling_recv, y_send, y_recv, up_send, up_recv, pass_send, pass_recv, w_send, w_recv,
 ):
     col = lax.axis_index("col")
     y, core = lax.div(col, 2), lax.rem(col, 2)
@@ -218,13 +219,15 @@
     sibling = {"col": 2 * y + 1 - core}
     along_y = [{"col": 2 * place[k] + core} for k in range(ny)]
     barrier = pltpu.get_barrier_semaphore()
-    greet(barrier, [sibling, *along_y[1:]])
+    n_col = partial.shape[0]
+    along_col = [{"col": lax.rem(col + k, n_col)} for k in range(1, n_col)]
+    greet(barrier, along_col)
     size, width = features.shape
     scale[...] = jnp.broadcast_to(degrees[...].astype(jnp.float32), (width, size)).T
     own_part[...] = bias[...] + jnp.dot(
         features[...], w_self[...], preferred_element_type=jnp.float32
     )
-    pl.semaphore_wait(barrier, ny)
+    pl.semaphore_wait(barrier, n_col - 1)
 
     started = []
 
@@ -289,11 +292,29 @@
         layer_out[here] = (preact * sigmoid_values).astype(layer_out.dtype)
         mean_rows[here] = mean
         grad_preact[here] = gradient
+    part_rows = width // n_col
+    for which, source in enumerate((features, mean_rows)):
+        product = lax.dot_general(
+            source[...], grad_preact[...], (((0,), (0,)), ((), ())), preferred_element_type=jnp.float32
+        ).astype(parts.dtype)
+        for c in range(n_col):
+            parts[c, which * part_rows : (which + 1) * part_rows] = product[
+                c * part_rows : (c + 1) * part_rows
+            ]
+    reduced = [
+        start(parts.at[lax.rem(col + k, n_col)], parts_arrived.at[k - 1], w_send, w_recv, k - 1, peer)
+        for k, peer in enumerate(along_col, 1)
+    ]
     for half in range(halves):
         for k in reversed(far_first):
             gathered[half, k].wait_recv()
             held = upward_rows.at[2 * lax.rem(y + ny - k, ny) + core, half]
             passed.append(start(held, held, pass_send, pass_recv, half * ny + k, sibling))
+    total = parts[col].astype(jnp.float32)
+    for k, each in enumerate(reduced):
+        each.wait_recv()
+        total = total + parts_arrived[k].astype(jnp.float32)
+    weight_sums[...] = total
     for each in passed:
         each.wait_recv()
     for each in started:
@@ -303,35 +324,32 @@
 
 
 def scatter_kernel(
-    transfers, order, n_parts, nx, nz, n_col, grad_scale, partial, features, mean_rows, grad_preact, w_self,
+    transfers, order, split, nx, nz, n_col, grad_scale, partial, weight_parts, grad_preact, w_self,
     moved_in, weight_sums,
-    total, arrived, parts, col_arrived, col_sums, z_arrived, x_sums, z_sums, all_sums,
-    load_sem, send_sem, recv_sem, c_send, c_recv, z_send, z_recv, x_send, x_recv, zz_send, zz_recv, cc_send, cc_recv,
+    arrived, self_grad, z_arrived, x_sums, z_sums,
+    news, send_sem, recv_sem, z_send, z_recv, x_send, x_recv, zz_send, zz_recv, cc_send, cc_recv,
 ):
     torus = Torus(nx, nz)
     col = lax.axis_index("col")
-    load = pltpu.make_async_copy(partial, total, load_sem)
-    load.start()
-    barrier = pltpu.get_barrier_semaphore()
+    cols = [lax.rem(col + k, n_col) for k in range(n_col)]
+    along_col = [{"col": c} for c in cols[1:]]
     along_z = [{"row": torus.row(0, k)} for k in range(1, nz)]
     along_x = [{"row": torus.row(k, 0)} for k in range(1, nx)]
-    cols = [lax.rem(col + k, n_col) for k in range(n_col)]
-    along_col = [{"col": c} for c in cols[1:]]
-    greet(barrier, along_z + along_x + along_col)
-    moved = jnp.dot(
-        row_order(grad_preact.shape[0]), grad_preact[...], preferred_element_type=jnp.float32
-    ).astype(jnp.bfloat16)
-    self_grad = lax.dot_general(
-        moved, w_self[...], (((1,), (1,)), ((), ())), preferred_element_type=jnp.float32
-    )
-    rows = w_self.shape[0] // n_col
-    for half, source in enumerate((features, mean_rows)):
-        product = lax.dot_general(
-            source[...], grad_preact[...], (((0,), (0,)), ((), ())), preferred_element_type=jnp.float32
-        ).astype(parts.dtype)
-        for c in range(n_col):
-            parts[c, half * rows : (half + 1) * rows] = product[c * rows : (c + 1) * rows]
-    pl.semaphore_wait(barrier, len(along_z) + len(along_x) + len(along_col))
+    z_next, x_next = [along_z[0], along_z[-1]], [along_x[0], along_x[-1]]
+    y_next = [{"col": cols[2]}, {"col": cols[-2]}]
+    sibling = {"col": col + 1 - 2 * lax.rem(col, 2)}
+    barrier = pltpu.get_barrier_semaphore()
+    greet(barrier, [*z_next, *x_next, *y_next, sibling])
+    rounds = [[*z_next, *x_next, *y_next], [*z_next, *y_next], z_next]
+
+    def tell(number):
+        greet(news.at[number], rounds[number])
+
+    def hear(number):
+        pl.semaphore_wait(news.at[number], len(rounds[number]))
+
+    pl.semaphore_wait(barrier, 7)
+    tell(0)
 
     started = []
 
@@ -349,28 +367,31 @@
         started[-1].start()
         return started[-1]
 
-    def reduce_along_col():
+    def pass_first(_):
+        hear(0)
+        tell(1)
+        moved = jnp.dot(
+            row_order(grad_preact.shape[0]), grad_preact[...], preferred_element_type=jnp.float32
+        ).astype(jnp.bfloat16)
+        self_grad[...] = lax.dot_general(
+            moved, w_self[...], (((1,), (1,)), ((), ())), preferred_element_type=jnp.float32
+        )
+
+    def pass_second(_):
+        hear(1)
+        tell(2)
+
+    def reduce_along_z(_):
+        hear(2)
         return [
-            start(parts.at[cols[k]], col_arrived.at[k - 1], c_send, c_recv, k - 1, peer)
-            for k, peer in enumerate(along_col, 1)
-        ]
-
-    def reduce_along_z(before):
-        for each in before:
-            each.wait_recv()
-        part = parts[col].astype(jnp.float32)
-        for k in range(n_col - 1):
-            part = part + col_arrived[k].astype(jnp.float32)
-        col_sums[...] = part.reshape(col_sums.shape)
-        return [
-            start(col_sums.at[lax.rem(torus.z + k, nz)], z_arrived.at[k - 1], z_send, z_recv, k - 1, peer)
+            start(weight_parts.at[lax.rem(torus.z + k, nz)], z_arrived.at[k - 1], z_send, z_recv, k - 1, peer)
             for k, peer in enumerate(along_z, 1)
         ]
 
     def reduce_along_x(before):
         for each in before:
             each.wait_recv()
-        part = col_sums[torus.z]
+        part = weight_parts[torus.z]
         for k in range(nz - 1):
             part = part + z_arrived[k]
         x_sums[torus.x] = part
@@ -394,16 +415,16 @@
     def gather_along_col(before):
         for each in before:
             each.wait_recv()
-        all_sums[col] = z_sums[...].reshape(all_sums.shape[1:])
+        weight_sums[col] = z_sums[...].reshape(weight_sums.shape[1:]).astype(weight_sums.dtype)
         return [
-            start(all_sums.at[col], all_sums.at[col], cc_send, cc_recv, k, peer)
+            start(weight_sums.at[col], weight_sums.at[col], cc_send, cc_recv, k, peer)
             for k, peer in enumerate(along_col)
         ]
 
-    def copy(index, node):
-        axis, sign, first, count, _ = transfers[index]
+    def carry(index, source):
+        axis, sign, _, count, _ = transfers[index]
         return start(
-            total.at[torus.row(node[1], node[2]), pl.ds(first, count)],
+            source,
             arrived.at[index, pl.ds(0, count)],
             send_sem,
             recv_sem,
@@ -411,47 +432,54 @@
             torus.neighbour(axis, -sign),
         )
 
-    sent = {}
-    pending = reduce_along_col()
-    steps = (reduce_along_z, reduce_along_x, gather_along_z, gather_along_col)
-    stages = {len(order) * (k + 2) // 7: step for k, step in enumerate(steps)}
-    load.wait()
-    for position, (node, brought, carried) in enumerate(reversed(order)):
-        if position in stages:
-            pending = stages[position](pending)
-        owner = torus.row(node[1], node[2])
+    def sum_of(node, carried):
+        _, first, full = split[node[0]]
+        value = partial[torus.row(node[1], node[2]), first : first + full].astype(jnp.float32)
         for index in reversed(carried):
-            first, count = transfers[index][2:4]
+            lead, count = transfers[index][2:4]
             sent[index].wait_recv()
-            if brought:
-                rows = pl.ds(first, count)
-                total[owner, rows] = (
-                    total[owner, rows].astype(jnp.float32)
-                    + arrived[index, :count].astype(jnp.float32)
-                ).astype(total.dtype)
-        for index in reversed(brought):
-            sent[index] = copy(index, node)
-
-    me = torus.row(0, 0)
-    sums = []
-    for (node, _, first_carried), (_, _, carried) in zip(order[:n_parts], order[n_parts:]):
-        carried = first_carried + carried
-        first = min(transfers[index][2] for index in carried)
-        full = max(transfers[index][2] + transfers[index][3] for index in carried) - first
-        part = total[me, first : first + full].astype(jnp.float32)
-        for index in carried:
-            lead, count = transfers[index][2:4]
             came = arrived[index, :count].astype(jnp.float32)
             if count < full:
                 filler = jnp.zeros((full - count, came.shape[1]), jnp.float32)
                 came = jnp.concatenate([came, filler] if lead == first else [filler, came], axis=0)
-            part = part + came
-        sums.append((first, part))
+            value = value + came
+        return value
+
+    sent = {}
+    pending = []
+    steps = [pass_first, pass_second, reduce_along_z, reduce_along_x, gather_along_z, gather_along_col]
+    n_parts = len(split)
+    inner = sum(1 for _, brought, carried in order if brought and carried)
+    stages = {inner * at // 100: step for at, step in zip(STAGES, steps)}
+    seen = 0
+    for node, brought, carried in reversed(order[2 * n_parts :]):
+        begin = split[node[0]][1]
+        if carried:
+            if seen in stages:
+                pending = stages[seen](pending)
+            seen += 1
+            full = split[node[0]][2]
+            home = next(index for index in carried if transfers[index][3] == full)
+            if len(carried) == 1:
+                sent[home].wait_recv()
+                arrived[home, :full] += partial[torus.row(node[1], node[2]), begin : begin + full]
+            else:
+                arrived[home, :full] = sum_of(node, carried).astype(arrived.dtype)
+        for index in reversed(brought):
+            first, count = transfers[index][2:4]
+            if carried:
+                source = arrived.at[home, pl.ds(first - begin, count)]
+            else:
+                source = partial.at[torus.row(node[1], node[2]), pl.ds(first, count)]
+            sent[index] = carry(index, source)
+
+    sums = []
+    for (node, _, first_carried), (_, _, carried) in zip(order[:n_parts], order[n_parts:]):
+        sums.append((split[node[0]][1], sum_of(node, first_carried + carried)))
     neighbour_sum = jnp.concatenate([part for _, part in sorted(sums, key=lambda pair: pair[0])], axis=0)
-    moved_in[...] = (self_grad + neighbour_sum).astype(moved_in.dtype)
+    moved_in[...] = (self_grad[...] + neighbour_sum).astype(moved_in.dtype)
     for each in pending:
         each.wait_recv()
-    weight_sums[...] = all_sums[...]
     for each in started:
         each.wait_send()
 
@@ -462,8 +490,122 @@
     ).astype(grad_in.dtype)
     rows = weight_sums.shape[1] // 2
     for c in range(weight_sums.shape[0]):
-        grad_self[c * rows : (c + 1) * rows] = weight_sums[c, :rows]
-        grad_neigh[c * rows : (c + 1) * rows] = weight_sums[c, rows:]
+        grad_self[c * rows : (c + 1) * rows] = weight_sums[c, :rows].astype(grad_self.dtype)
+        grad_neigh[c * rows : (c + 1) * rows] = weight_sums[c, rows:].astype(grad_neigh.dtype)
+
+
+def array(dtype, *shape):
+    return jax.ShapeDtypeStruct(shape, dtype)
+
+
+def local(mib):
+    return pltpu.CompilerParams(vmem_limit_bytes=mib << 20)
+
+
+def remote(identity, mib):
+    return pltpu.CompilerParams(
+        collective_id=identity, has_side_effects=True, vmem_limit_bytes=mib << 20
+    )
+
+
+def gather_panel(features, nx, nz, split, identity=0):
+    size, width = features.shape
+    transfers, order = torus_plan(nx, nz, split)
+    copies = len(transfers)
+    return pl.pallas_call(
+        functools.partial(gather_kernel, transfers, order, nx, nz),
+        name="gather_panel",
+        out_shape=array(jnp.bfloat16, nx * nz, size, width),
+        in_specs=[VMEM],
+        out_specs=ANY,
+        scratch_shapes=[
+            pltpu.VMEM((size, width), jnp.bfloat16),
+            pltpu.SemaphoreType.DMA,
+            pltpu.SemaphoreType.DMA((copies,)),
+            pltpu.SemaphoreType.DMA((copies,)),
+        ],
+        compiler_params=remote(identity, 4),
+    )(features)
+
+
+def middle(partial, features, grad_out, degrees, w_self, w_neigh, bias, identity=1):
+    bf16, f32 = jnp.bfloat16, jnp.float32
+    dma = pltpu.SemaphoreType.DMA
+    size, width = features.shape
+    n_col, halves = partial.shape[:2]
+    ny = n_col // 2
+    return pl.pallas_call(
+        middle_kernel,
+        name="middle",
+        out_shape=(
+            array(bf16, size, width),
+            array(bf16, size, width),
+            array(bf16, n_col, halves, TILE, width),
+            array(f32, 2 * width // n_col, width),
+        ),
+        in_specs=[VMEM] * 7,
+        out_specs=(VMEM, VMEM, ANY, VMEM),
+        scratch_shapes=[
+            pltpu.VMEM((size, width), f32),
+            pltpu.VMEM((size, width), f32),
+            pltpu.VMEM((ny, halves, TILE, width), bf16),
+            pltpu.VMEM((ny - 1, halves, TILE, width), bf16),
+            pltpu.VMEM((ny - 1, halves, TILE, width), bf16),
+            pltpu.VMEM((halves, TILE, width), f32),
+            pltpu.VMEM((halves, TILE, width), bf16),
+            pltpu.VMEM((size, width), bf16),
+            pltpu.VMEM((n_col, 2 * width // n_col, width), bf16),
+            pltpu.VMEM((n_col - 1, 2 * width // n_col, width), bf16),
+            dma((halves,)),
+        ]
+        + [dma((ny * halves,))] * 2
+        + [dma(((ny - 1) * halves,))] * 4
+        + [dma((ny * halves,))] * 2
+        + [dma((n_col - 1,))] * 2,
+        compiler_params=remote(identity, 16),
+    )(
+        partial,
+        features,
+        grad_out,
+        degrees[None, :],
+        w_self,
+        w_neigh,
+        bias[None, :],
+    )
+
+
+def scatter_panel(spread, weight_parts, grad_preact, w_self, nx, nz, n_col, split, identity=2):
+    bf16, f32 = jnp.bfloat16, jnp.float32
+    dma = pltpu.SemaphoreType.DMA
+    size, width = grad_preact.shape
+    transfers, order = torus_plan(nx, nz, split)
+    copies = len(transfers)
+    grad_scale = 1.0 / math.sqrt(size * nx * nz * n_col)
+    grad_rows = 2 * width // n_col
+    z_rows = grad_rows // nz
+    others = n_col - 1
+    return pl.pallas_call(
+        functools.partial(scatter_kernel, transfers, order, split, nx, nz, n_col, grad_scale),
+        name="scatter_panel",
+        out_shape=(array(bf16, size, width), array(bf16, n_col, grad_rows, width)),
+        in_specs=[VMEM, VMEM, VMEM, VMEM],
+        out_specs=(VMEM, VMEM),
+        scratch_shapes=[
+            pltpu.VMEM((copies, max(part[2] for part in split), width), bf16),
+            pltpu.VMEM((size, width), f32),
+            pltpu.VMEM((nz - 1, z_rows, width), f32),
+            pltpu.VMEM((nx, z_rows, width), f32),
+            pltpu.VMEM((nz, z_rows, width), f32),
+            pltpu.SemaphoreType.REGULAR((3,)),
+            dma((copies,)),
+            dma((copies,)),
+        ]
+        + [dma((nz - 1,))] * 2
+        + [dma((nx - 1,))] * 2
+        + [dma((nz - 1,))] * 2
+        + [dma((others,))] * 2,
+        compiler_params=remote(identity, 24),
+    )(spread, weight_parts.reshape(nz, z_rows, width), grad_preact, w_self)
 
 
 def shards(features, grad_out, degrees, w_self, w_neigh, bias, tile_slots, tile_count, tile_masks):
@@ -471,36 +613,14 @@
     n_row, n_col = lax.axis_size("row"), lax.axis_size("col")
     nx, nz = 4, n_row // 4
     split = [("xz", 0, 48), ("xz", 48, 48), ("zx", 96, 80), ("zx", 176, 80)]
-    transfers, order = torus_plan(nx, nz, split)
-    copies = len(transfers)
     bf16, f32 = jnp.bfloat16, jnp.float32
     dma = pltpu.SemaphoreType.DMA
     slots, count, masks = tile_slots[0, 0], tile_count[0], tile_masks[0, 0]
     block_rows = size * n_col // TILE
     block_columns = size * n_row // TILE
     halves = size // TILE
-    ny = n_col // 2
-
-    def array(dtype, *shape):
-        return jax.ShapeDtypeStruct(shape, dtype)
-
-    def local(mib):
-        return pltpu.CompilerParams(vmem_limit_bytes=mib << 20)
-
-    def remote(identity, mib):
-        return pltpu.CompilerParams(
-            collective_id=identity, has_side_effects=True, vmem_limit_bytes=mib << 20
-        )
-
-    panel = pl.pallas_call(
-        functools.partial(gather_kernel, transfers, order, nx, nz),
-        name="gather_panel",
-        out_shape=array(bf16, n_row, size, width),
-        in_specs=[VMEM],
-        out_specs=ANY,
-        scratch_shapes=[pltpu.VMEM((size, width), bf16), dma, dma((copies,)), dma((copies,))],
-        compiler_params=remote(0, 4),
-    )(features)
+
+    panel = gather_panel(features, nx, nz, split)
 
     partial = pl.pallas_call(
         aggregate_kernel,
@@ -512,39 +632,8 @@
         compiler_params=local(16),
     )(slots, count, masks, panel.reshape(block_columns, TILE, width))
 
-    layer_in, mean_rows, grad_preact, upward_rows = pl.pallas_call(
-        middle_kernel,
-        name="middle",
-        out_shape=(
-            array(bf16, size, width),
-            array(bf16, size, width),
-            array(bf16, size, width),
-            array(bf16, n_col, halves, TILE, width),
-        ),
-        in_specs=[VMEM] * 7,
-        out_specs=(VMEM, VMEM, VMEM, ANY),
-        scratch_shapes=[
-            pltpu.VMEM((size, width), f32),
-            pltpu.VMEM((size, width), f32),
-            pltpu.VMEM((ny, halves, TILE, width), bf16),
-            pltpu.VMEM((ny - 1, halves, TILE, width), bf16),
-            pltpu.VMEM((ny - 1, halves, TILE, width), bf16),
-            pltpu.VMEM((halves, TILE, width), f32),
-            pltpu.VMEM((halves, TILE, width), bf16),
-            dma((halves,)),
-        ]
-        + [dma((ny * halves,))] * 2
-        + [dma(((ny - 1) * halves,))] * 4
-        + [dma((ny * halves,))] * 2,
-        compiler_params=remote(1, 16),
-    )(
-        partial.reshape(n_col, halves, TILE, width),
-        features,
-        grad_out,
-        degrees[None, :],
-        w_self,
-        w_neigh,
-        bias[None, :],
+    layer_in, grad_preact, upward_rows, weight_parts = middle(
+        partial.reshape(n_col, halves, TILE, width), features, grad_out, degrees, w_self, w_neigh, bias
     )
 
     spread, layer_out = pl.pallas_call(
@@ -557,37 +646,9 @@
         compiler_params=local(24),
     )(slots, count, masks, upward_rows.reshape(block_rows, TILE, width), layer_in)
 
-    grad_scale = 1.0 / math.sqrt(size * n_row * n_col)
-    grad_rows = 2 * width // n_col
-    z_rows = grad_rows // nz
-    others = n_col - 1
-    moved_in, weight_sums = pl.pallas_call(
-        functools.partial(scatter_kernel, transfers, order, len(split), nx, nz, n_col, grad_scale),
-        name="scatter_panel",
-        out_shape=(array(bf16, size, width), array(f32, n_col, grad_rows, width)),
-        in_specs=[ANY, VMEM, VMEM, VMEM, VMEM],
-        out_specs=(VMEM, VMEM),
-        scratch_shapes=[
-            pltpu.VMEM((n_row, size, width), bf16),
-            pltpu.VMEM((copies, max(part[2] for part in split), width), bf16),
-            pltpu.VMEM((n_col, grad_rows, width), bf16),
-            pltpu.VMEM((others, grad_rows, width), bf16),
-            pltpu.VMEM((nz, z_rows, width), f32),
-            pltpu.VMEM((nz - 1, z_rows, width), f32),
-            pltpu.VMEM((nx, z_rows, width), f32),
-            pltpu.VMEM((nz, z_rows, width), f32),
-            pltpu.VMEM((n_col, grad_rows, width), f32),
-            dma,
-            dma((copies,)),
-            dma((copies,)),
-        ]
-        + [dma((others,))] * 2
-        + [dma((nz - 1,))] * 2
-        + [dma((nx - 1,))] * 2
-        + [dma((nz - 1,))] * 2
-        + [dma((others,))] * 2,
-        compiler_params=remote(2, 24),
-    )(spread.reshape(n_row, size, width), features, mean_rows, grad_preact, w_self)
+    moved_in, weight_sums = scatter_panel(
+        spread.reshape(n_row, size, width), weight_parts, grad_preact, w_self, nx, nz, n_col, split
+    )
 
     grad_in, grad_self, grad_neigh = pl.pallas_call(
         finish_kernel,

time: 112 us -> 110 us (0.982)
  Pallas kernels: 109 us -> 107 us
    pallas_call x3, Pallas kernels: 102 us -> 100 us  [the longest x1 42.4 us: scatter_panel(): pl.pallas_call(functools.partial(scatter_kernel, transfers, order, split,...]
where the time goes in v3:
time: 110 us; the launch traced here: 109 us
  Pallas kernels  107 us (97%)
  between operations  1.56 us (1%)
    pallas_call x1, Pallas kernels, scatter_panel(): pl.pallas_call(functools.partial(scatter_kernel, transfers, order, split,...  42.4 us
    pallas_call x1, Pallas kernels, gather_panel(): pl.pallas_call(functools.partial(gather_kernel, transfers, order, nx, nz)...  37 us
    pallas_call x1, Pallas kernels, middle(): pl.pallas_call(middle_kernel, name='middle', out_shape=(array(bf16, size,...  20.8 us
    pallas_call x1, Pallas kernels, shards(): pl.pallas_call(spread_kernel, name='spread', out_shape=(array(bf16, block...  3.27 us
    pallas_call x1, Pallas kernels, shards(): pl.pallas_call(aggregate_kernel, name='aggregate', out_shape=array(bf16,...  2.36 us

profile of v3, /device:TPU:8, one launch (start us, length us, event | category | flops | bytes accessed | tf_op | source)
XLA Modules:
  0.0 109.2 jit_solution(5808300116820378859)
XLA Ops:
  0.6 0.0 copy-start
  1.4 0.0 copy-start.1
  1.4 0.9 copy-done.1
  2.3 0.0 copy-start.6
  2.3 37.0 %gather_panel.1 = bf16[32,256,256]{2,1,0:T(8,128)(2,1)S(1)} custom-call(bf16[256,256]{1,0:T(8,128)(2,1)S(1)} %copy-done.1), custom_call_target="tpu_custom_call" | custom-call | tf_op jit(solution)/shard_map/gather_panel/pallas_call | solution.py:515
  39.3 0.0 copy-start.2
  39.3 0.0 copy-start.3
  39.3 0.0 copy-start.4
  39.4 0.0 copy-start.5
  39.4 0.0 copy-start.7
  39.4 0.0 copy-start.8
  39.4 0.0 copy-done
  39.4 0.0 copy-done.6
  39.4 2.4 %aggregate.1 = bf16[16,128,256]{2,1,0:T(8,128)(2,1)S(1)} custom-call(s32[176]{0:T(256)S(1)} %bitcast.19, s32[1]{0:T(128)} %bitcast.10.count, s32[176,16,128]{2,1,0:T(8,128)S(1)} %bitcast.13, bf16[64,128,256]{2,1,0:T(8,128)(2,1)S(1)} %bitcast.12), custom_call_target="tpu_custom_call" | custom-call | tf_op jit(solution)/shard_map/aggregate/pallas_call | solution.py:625
  41.8 0.0 copy-done.2
  41.8 0.0 copy-done.3
  41.8 0.0 copy-done.4
  41.8 0.0 copy-done.5
  41.8 0.0 copy-done.7
  41.8 0.0 copy-done.8
  41.8 20.8 %middle.1 = (bf16[256,256]{1,0:T(8,128)(2,1)S(1)}, bf16[256,256]{1,0:T(8,128)(2,1)S(1)}, bf16[8,2,128,256]{3,2,1,0:T(8,128)(2,1)S(1)}, f32[64,256]{1,0:T(8,128)S(1)}) custom-call(bf16[8,2,128,256]{3,2,1,0:T(8,128)(2,1)S(1)} %bitcast.16, bf16[256,256]{1,0:T(8,128)(2,1)S(1)} %copy-done.2, bf16[256,256]{1,0:T(8,128)(2,1)S(1)} %copy-done.4, ...), custom_call_target="tpu_custom_call" | custom-call | tf_op jit(solution)/shard_map/middle/pallas_call | solution.py:537
  62.6 3.3 %spread.1 = (bf16[64,128,256]{2,1,0:T(8,128)(2,1)S(1)}, bf16[256,256]{1,0:T(8,128)(2,1)}) custom-call(s32[176]{0:T(256)S(1)} %bitcast.20, s32[1]{0:T(128)} %bitcast.11.count, s32[176,16,128]{2,1,0:T(8,128)S(1)} %bitcast.14, bf16[16,128,256]{2,1,0:T(8,128)(2,1)S(1)} %bitcast.17, bf16[256,256]{1,0:T(8,128)(2,1)S(1)} %get-tuple-element.16.layer_in), custom_call_target="tpu_custom_call" | custom-call | tf_op jit(solution)/shard_map/spread/pallas_call | solution.py:639
  65.9 42.4 %scatter_panel.1 = (bf16[256,256]{1,0:T(8,128)(2,1)S(1)}, bf16[8,64,256]{2,1,0:T(8,128)(2,1)S(1)}) custom-call(bf16[32,256,256]{2,1,0:T(8,128)(2,1)S(1)} %bitcast.15, f32[8,8,256]{2,1,0:T(8,128)S(1)} %bitcast.18, bf16[256,256]{1,0:T(8,128)(2,1)S(1)} %get-tuple-element.20.grad_preact, bf16[256,256]{1,0:T(8,128)(2,1)S(1)} %copy-done.3), custom_call_target="tpu_custom_call" | custom-call | tf_op jit(solution)/shard_map/scatter_panel/pallas_call | solution.py:587
  108.3 1.0 finish.1
Async XLA Ops:
  0.6 38.8 %copy-start = (s32[1,1,176,16,128]{4,3,2,1,0:T(8,128)S(1)}, s32[1,1,176,16,128]{4,3,2,1,0:T(8,128)}, u32[]{:S(2)}) copy-start(s32[1,1,176,16,128]{4,3,2,1,0:T(8,128)} %param.17) | copy-start | bytes 4325380
  1.4 0.9 copy-start.1
  2.3 37.1 %copy-start.6 = (s32[1,1,176]{2,1,0:T(1,128)S(1)}, s32[1,1,176]{2,1,0:T(1,128)}, u32[]{:S(2)}) copy-start(s32[1,1,176]{2,1,0:T(1,128)} %param.15) | copy-start | bytes 2116
  39.3 2.5 %copy-start.2 = (bf16[256,256]{1,0:T(8,128)(2,1)S(1)}, bf16[256,256]{1,0:T(8,128)(2,1)}, u32[]{:S(2)}) copy-start(bf16[256,256]{1,0:T(8,128)(2,1)} %features.3) | copy-start | bytes 393220
  39.3 2.5 %copy-start.3 = (bf16[256,256]{1,0:T(8,128)(2,1)S(1)}, bf16[256,256]{1,0:T(8,128)(2,1)}, u32[]{:S(2)}) copy-start(bf16[256,256]{1,0:T(8,128)(2,1)} %w_self.3) | copy-start | bytes 393220
  39.3 2.5 %copy-start.4 = (bf16[256,256]{1,0:T(8,128)(2,1)S(1)}, bf16[256,256]{1,0:T(8,128)(2,1)}, u32[]{:S(2)}) copy-start(bf16[256,256]{1,0:T(8,128)(2,1)} %grad_out.1) | copy-start | bytes 393220
  39.4 2.5 %copy-start.5 = (bf16[256,256]{1,0:T(8,128)(2,1)S(1)}, bf16[256,256]{1,0:T(8,128)(2,1)}, u32[]{:S(2)}) copy-start(bf16[256,256]{1,0:T(8,128)(2,1)} %w_neigh.1) | copy-start | bytes 393220
  39.4 2.5 %copy-start.7 = (s32[256]{0:T(256)S(1)}, s32[256]{0:T(256)}, u32[]{:S(2)}) copy-start(s32[256]{0:T(256)} %param.11) | copy-start | bytes 3076
  39.4 2.5 %copy-start.8 = (f32[256]{0:T(256)S(1)}, f32[256]{0:T(256)}, u32[]{:S(2)}) copy-start(f32[256]{0:T(256)} %param.14) | copy-start | bytes 3076

commit v4 on v3

v4 whole, which is shorter than its diff:
```python
import functools
import heapq
import math

import jax
import jax.numpy as jnp
from jax import lax
from jax.experimental import pallas as pl
from jax.experimental.pallas import tpu as pltpu
from jax.sharding import PartitionSpec as P

MESH = pl.DeviceIdType.MESH
SMEM = pl.BlockSpec(memory_space=pltpu.SMEM)
VMEM = pl.BlockSpec(memory_space=pltpu.VMEM)
ANY = pl.BlockSpec(memory_space=pl.ANY)
TILE = 128
UNROLL = 16
STAGES = (0, 2, 18, 38, 58)


def torus_plan(nx, nz, split, latency=4.0, rate=0.0085):
    size = {"x": nx, "z": nz}
    transfers, order = [], []
    free, heap = {}, []

    def wrap(d, n):
        d %= n
        return d - n if d > n // 2 else d

    def send(now, node, axis, sign, first, count):
        offset = {"x": node[1], "z": node[2]}
        offset[axis] = wrap(offset[axis] - sign, size[axis])
        index = len(transfers)
        transfers.append((axis, sign, first, count, (node[0], offset["x"], offset["z"])))
        start = max(now, free.get((axis, sign), 0.0))
        free[axis, sign] = start + count * rate
        heapq.heappush(heap, (free[axis, sign] + latency, index))
        entries[node][1].append(index)

    def forward(now, node, phases="pq"):
        part = node[0]
        (p, q), begin, full = split[part]
        offset = {"x": node[1], "z": node[2]}
        dp, dq = offset[p], offset[q]
        half_p, half_q = size[p] // 2, size[q] // 2
        lower = (full // 2 + 15) // 16 * 16
        for sign in (1, -1) if "p" in phases else ():
            if dq == 0 and (dp == 0 or -dp * sign > 0) and dp != half_p:
                if abs(dp) + 1 < half_p:
                    send(now, node, p, sign, begin, full)
                elif sign == 1:
                    send(now, node, p, sign, begin, lower)
                else:
                    send(now, node, p, sign, begin + lower, full - lower)
        for sign in (1, -1) if "q" in phases else ():
            if (dq == 0 or -dq * sign > 0) and dq != half_q:
                if abs(dq) + 1 < half_q or (0 <= dp < half_p) == (sign == 1):
                    send(now, node, q, sign, begin, full)

    got = {}
    entries = {(part, 0, 0): ([], []) for part in range(len(split))}
    roots = []
    for phases in "pq":
        for part in range(len(split)):
            forward(0.0, (part, 0, 0), phases)
            roots.append(((part, 0, 0), [], entries[part, 0, 0][1]))
            entries[part, 0, 0] = ([], [])
    while heap:
        now, index = heapq.heappop(heap)
        count, node = transfers[index][3:]
        entries.setdefault(node, ([], []))[0].append(index)
        got[node] = got.get(node, 0) + count
        if got[node] == split[node[0]][2]:
            order.append(node)
            forward(now, node)
    return transfers, roots + [(node, *entries[node]) for node in order]


class Torus:
    def __init__(self, nx, nz):
        self.nx, self.nz = nx, nz
        row = lax.axis_index("row")
        self.x, self.z = lax.rem(row, nx), lax.div(row, nx)

    def row(self, dx, dz):
        x = lax.rem(self.x + (dx + self.nx), self.nx)
        z = lax.rem(self.z + (dz + self.nz), self.nz)
        return z * self.nx + x

    def neighbour(self, axis, sign):
        return {"row": self.row(sign, 0) if axis == "x" else self.row(0, sign)}


def greet(barrier, peers):
    for peer in peers:
        pl.semaphore_signal(barrier, inc=1, device_id=peer, device_id_type=MESH)


def row_order(size):
    place = lax.broadcasted_iota(jnp.int32, (size, size), 0)
    node = lax.broadcasted_iota(jnp.int32, (size, size), 1)
    within = place & (TILE - 1)
    source = (place - within) + ((within & 15) << 3) + (within >> 4)
    return jnp.where(source == node, 1.0, 0.0).astype(jnp.bfloat16)


class Sender:
    def __init__(self):
        self.started = []

    def __call__(self, source, target, sends, recvs, k, peer):
        copy = pltpu.make_async_remote_copy(
            src_ref=source,
            dst_ref=target,
            send_sem=sends.at[k],
            recv_sem=recvs.at[k],
            device_id=peer,
            device_id_type=MESH,
        )
        copy.start()
        self.started.append(copy)
        return copy


def gather_phase(start, torus, transfers, order, own, panel, send_sem, recv_sem, sent):
    for node, brought, carried in order:
        for index in brought:
            sent[index].wait_recv()
        origin = torus.row(node[1], node[2])
        for index in carried:
            axis, sign, first, count, _ = transfers[index]
            rows = pl.ds(first, count)
            sent[index] = start(
                panel.at[origin, rows] if brought else own.at[rows],
                panel.at[origin, rows],
                send_sem,
                recv_sem,
                index,
                torus.neighbour(axis, sign),
            )
    return sent


def unpack(words):
    return jnp.concatenate(
        [((words >> bit) & 1).astype(jnp.float32).astype(jnp.bfloat16) for bit in range(8)], axis=0
    )


def chain_tiles(slots, before, masks, sums, product):
    def group(index, _):
        for u in range(UNROLL):
            tile = index * UNROLL + u
            sums[tile + 1] = sums[before[tile]] + product(slots[tile], unpack(masks[tile]))
        return 0

    lax.fori_loop(0, masks.shape[0] // UNROLL, group, 0)


def middle_phase(
    start, col, partial, features, grad_out, w_neigh, layer_out, grad_preact, upward_rows, weight_parts,
    own_part, scale, from_sibling, joined, arrived, own_sum, upward, mean_rows, parts, parts_arrived,
    keep_sem, sibling_send, sibling_recv, y_send, y_recv, up_send, up_recv, pass_send, pass_recv, w_send, w_recv,
):
    y, core = lax.div(col, 2), lax.rem(col, 2)
    ny, halves, rows = from_sibling.shape[:3]
    n_col = 2 * ny
    width = features.shape[1]
    place = [lax.rem(y + k, ny) for k in range(ny)]
    far_first = sorted(range(1, ny), key=lambda k: -min(k, ny - k))
    sibling = {"col": 2 * y + 1 - core}
    along_y = [{"col": 2 * place[k] + core} for k in range(ny)]
    along_col = [{"col": lax.rem(col + k, n_col)} for k in range(1, n_col)]
    pieces = [(half, k) for half in range(halves) for k in (*far_first, 0)]
    shared = {}
    for half, k in pieces:
        shared[half, k] = start(
            partial.at[4 * place[k] + 2 * (1 - core) + half], from_sibling.at[k, half],
            sibling_send, sibling_recv, half * ny + k, sibling,
        )
    exchanged = {}
    for half, k in pieces:
        shared[half, k].wait_recv()
        both = partial[4 * place[k] + 2 * core + half].astype(jnp.float32)
        both = both + from_sibling[k, half].astype(jnp.float32)
        if k == 0:
            own_sum[half] = both
        else:
            joined[k - 1, half] = both.astype(joined.dtype)
            exchanged[half, k] = start(
                joined.at[k - 1, half], arrived.at[k - 1, half],
                y_send, y_recv, half * (ny - 1) + k - 1, along_y[k],
            )
    gathered, passed, kept = {}, [], []
    for half in range(halves):
        summed = own_sum[half]
        for k in far_first:
            exchanged[half, k].wait_recv()
            summed = summed + arrived[k - 1, half].astype(jnp.float32)
        here = slice(half * rows, (half + 1) * rows)
        mean = (summed / scale[here]).astype(mean_rows.dtype)
        preact = own_part[here] + jnp.dot(mean, w_neigh[...], preferred_element_type=jnp.float32)
        sigmoid_values = jax.nn.sigmoid(preact)
        gradient = (
            grad_out[here].astype(jnp.float32) * sigmoid_values * (1.0 + preact * (1.0 - sigmoid_values))
        ).astype(grad_preact.dtype)
        sent_up = lax.dot_general(
            gradient, w_neigh[...], (((1,), (1,)), ((), ())), preferred_element_type=jnp.float32
        )
        upward[half] = (sent_up / scale[here]).astype(upward.dtype)
        target = upward_rows.at[2 * col + half]
        for k in far_first:
            gathered[half, k] = start(
                upward.at[half], target, up_send, up_recv, half * (ny - 1) + k - 1, along_y[k]
            )
        passed.append(start(upward.at[half], target, pass_send, pass_recv, half * ny, sibling))
        kept.append(pltpu.make_async_copy(upward.at[half], target, keep_sem.at[half]))
        kept[-1].start()
        layer_out[here] = (preact * sigmoid_values).astype(layer_out.dtype)
        mean_rows[here] = mean
        grad_preact[here] = gradient
    part_rows = width // n_col
    for which, source in enumerate((features, mean_rows)):
        product = lax.dot_general(
            source[...], grad_preact[...], (((0,), (0,)), ((), ())), preferred_element_type=jnp.float32
        ).astype(parts.dtype)
        for c in range(n_col):
            parts[c, which * part_rows : (which + 1) * part_rows] = product[
                c * part_rows : (c + 1) * part_rows
            ]
    reduced = [
        start(parts.at[lax.rem(col + k, n_col)], parts_arrived.at[k - 1], w_send, w_recv, k - 1, peer)
        for k, peer in enumerate(along_col, 1)
    ]
    for half in range(halves):
        for k in reversed(far_first):
            gathered[half, k].wait_recv()
            held = upward_rows.at[4 * lax.rem(y + ny - k, ny) + 2 * core + half]
            passed.append(start(held, held, pass_send, pass_recv, half * ny + k, sibling))
    total = parts[col].astype(jnp.float32)
    for k, each in enumerate(reduced):
        each.wait_recv()
        total = total + parts_arrived[k].astype(jnp.float32)
    weight_parts[...] = total.reshape(weight_parts.shape)
    for each in passed:
        each.wait_recv()
    for each in kept:
        each.wait()


def scatter_phase(
    start, torus, col, transfers, order, split, n_col, grad_scale, partial, weight_parts, grad_preact, w_self,
    moved_in, weight_sums, arrived, self_grad, z_arrived, x_sums, z_sums,
    send_sem, recv_sem, z_send, z_recv, x_send, x_recv, zz_send, zz_recv, cc_send, cc_recv,
):
    nx, nz = torus.nx, torus.nz
    along_col = [{"col": lax.rem(col + k, n_col)} for k in range(1, n_col)]
    along_z = [{"row": torus.row(0, k)} for k in range(1, nz)]
    along_x = [{"row": torus.row(k, 0)} for k in range(1, nx)]

    def multiply_self(before):
        moved = jnp.dot(
            row_order(grad_preact.shape[0]), grad_preact[...], preferred_element_type=jnp.float32
        ).astype(jnp.bfloat16)
        self_grad[...] = lax.dot_general(
            moved, w_self[...], (((1,), (1,)), ((), ())), preferred_element_type=jnp.float32
        )
        return before

    def reduce_along_z(_):
        return [
            start(weight_parts.at[lax.rem(torus.z + k, nz)], z_arrived.at[k - 1], z_send, z_recv, k - 1, peer)
            for k, peer in enumerate(along_z, 1)
        ]

    def reduce_along_x(before):
        for each in before:
            each.wait_recv()
        part = weight_parts[torus.z]
        for k in range(nz - 1):
            part = part + z_arrived[k]
        x_sums[torus.x] = part
        return [
            start(x_sums.at[torus.x], x_sums.at[torus.x], x_send, x_recv, k, peer)
            for k, peer in enumerate(along_x)
        ]

    def gather_along_z(before):
        for each in before:
            each.wait_recv()
        part = x_sums[0]
        for k in range(1, nx):
            part = part + x_sums[k]
        z_sums[torus.z] = part * grad_scale
        return [
            start(z_sums.at[torus.z], z_sums.at[torus.z], zz_send, zz_recv, k, peer)
            for k, peer in enumerate(along_z)
        ]

    def gather_along_col(before):
        for each in before:
            each.wait_recv()
        weight_sums[col] = z_sums[...].reshape(weight_sums.shape[1:]).astype(weight_sums.dtype)
        return [
            start(weight_sums.at[col], weight_sums.at[col], cc_send, cc_recv, k, peer)
            for k, peer in enumerate(along_col)
        ]

    def carry(index, source):
        axis, sign, _, count, _ = transfers[index]
        return start(
            source,
            arrived.at[index, pl.ds(0, count)],
            send_sem,
            recv_sem,
            index,
            torus.neighbour(axis, -sign),
        )

    def sum_of(node, carried):
        _, first, full = split[node[0]]
        value = partial[torus.row(node[1], node[2]), first : first + full].astype(jnp.float32)
        for index in reversed(carried):
            lead, count = transfers[index][2:4]
            sent[index].wait_recv()
            came = arrived[index, :count].astype(jnp.float32)
            if count < full:
                filler = jnp.zeros((full - count, came.shape[1]), jnp.float32)
                came = jnp.concatenate([came, filler] if lead == first else [filler, came], axis=0)
            value = value + came
        return value

    sent = {}
    pending = []
    steps = [reduce_along_z, multiply_self, reduce_along_x, gather_along_z, gather_along_col]
    n_parts = len(split)
    inner = sum(1 for _, brought, carried in order if brought and carried)
    stages = {inner * at // 100: step for at, step in zip(STAGES, steps)}
    seen = 0
    for node, brought, carried in reversed(order[2 * n_parts :]):
        begin = split[node[0]][1]
        if carried:
            if seen in stages:
                pending = stages[seen](pending)
            seen += 1
            full = split[node[0]][2]
            home = next(index for index in carried if transfers[index][3] == full)
            if len(carried) == 1:
                sent[home].wait_recv()
                arrived[home, :full] += partial[torus.row(node[1], node[2]), begin : begin + full]
            else:
                arrived[home, :full] = sum_of(node, carried).astype(arrived.dtype)
        for index in reversed(brought):
            first, count = transfers[index][2:4]
            if carried:
                source = arrived.at[home, pl.ds(first - begin, count)]
            else:
                source = partial.at[torus.row(node[1], node[2]), pl.ds(first, count)]
            sent[index] = carry(index, source)

    sums = []
    for (node, _, first_carried), (_, _, carried) in zip(order[:n_parts], order[n_parts:]):
        sums.append((split[node[0]][1], sum_of(node, first_carried + carried)))
    neighbour_sum = jnp.concatenate([part for _, part in sorted(sums, key=lambda pair: pair[0])], axis=0)
    moved_in[...] = (self_grad[...] + neighbour_sum).astype(moved_in.dtype)
    for each in pending:
        each.wait_recv()


def layer_kernel(
    transfers, order, split, nx, nz, n_col, grad_scale,
    slots, row_chain, column_chain,
    features_in, grad_out_in, degrees_in, w_self_in, w_neigh_in, bias_in, masks_in,
    layer_out, moved_in, weight_sums,
    features, grad_out, degrees, w_self, w_neigh, bias, masks,
    own, panel, sums, partial, grad_preact, upward_rows, weight_parts, spread,
    own_part, scale, from_sibling, joined, y_arrived, own_sum, upward, mean_rows, parts, parts_arrived,
    arrived, self_grad, z_arrived, x_sums, z_sums,
    load_sem, own_sem, ring_send, ring_recv, back_send, back_recv, keep_sem, *sems,
):
    torus = Torus(nx, nz)
    col = lax.axis_index("col")
    start = Sender()
    loads = [
        pltpu.make_async_copy(source, target, load_sem.at[k])
        for k, (source, target) in enumerate(
            (
                (features_in, features),
                (w_self_in, w_self),
                (degrees_in, degrees),
                (bias_in, bias),
                (grad_out_in, grad_out),
                (w_neigh_in, w_neigh),
                (masks_in, masks),
            )
        )
    ]
    for each in loads:
        each.start()
    barrier = pltpu.get_barrier_semaphore()
    around = [torus.neighbour(axis, sign) for axis in "xz" for sign in (1, -1)]
    around.append({"col": col + 1 - 2 * lax.rem(col, 2)})
    around += [{"col": lax.rem(col + k, n_col)} for k in range(2, n_col, 2)]
    greet(barrier, around)
    loads[0].wait()
    own[...] = jnp.dot(
        row_order(own.shape[0]), features[...], preferred_element_type=jnp.float32
    ).astype(own.dtype)
    keep = pltpu.make_async_copy(own, panel.at[torus.row(0, 0)], own_sem)
    keep.start()
    pl.semaphore_wait(barrier, len(around))

    roots = 2 * len(split)
    sent = gather_phase(start, torus, transfers, order[:roots], own, panel, ring_send, ring_recv, {})
    size, width = features.shape
    for each in loads[1:]:
        each.wait()
    scale[...] = jnp.broadcast_to(degrees[...].astype(jnp.float32), (width, size)).T
    own_part[...] = bias[...] + jnp.dot(
        features[...], w_self[...], preferred_element_type=jnp.float32
    )
    sums[0] = jnp.zeros(sums.shape[1:], sums.dtype)
    gather_phase(start, torus, transfers, order[roots:], own, panel, ring_send, ring_recv, sent)
    keep.wait()

    n_tiles, block_rows = masks.shape[0], partial.shape[0]
    in_row = size // TILE

    def aggregate(slot, bits):
        block = lax.div(slot, block_rows)
        source = panel[lax.div(block, in_row), pl.ds(lax.rem(block, in_row) * TILE, TILE)]
        return lax.dot_general(bits, source, (((0,), (0,)), ((), ())), preferred_element_type=jnp.float32)

    chain_tiles(slots, row_chain, masks, sums, aggregate)
    for k in range(block_rows):
        partial[k] = sums[row_chain[n_tiles + k]].astype(partial.dtype)

    middle_phase(
        start, col, partial, features, grad_out, w_neigh, layer_out, grad_preact, upward_rows, weight_parts,
        own_part, scale, from_sibling, joined, y_arrived, own_sum, upward, mean_rows, parts, parts_arrived,
        keep_sem, *sems[:10],
    )

    def spread_tile(slot, bits):
        return jnp.dot(bits, upward_rows[lax.rem(slot, block_rows)], preferred_element_type=jnp.float32)

    chain_tiles(slots, column_chain, masks, sums, spread_tile)
    for k in range(spread.shape[0] * in_row):
        here = slice(k % in_row * TILE, (k % in_row + 1) * TILE)
        spread[k // in_row, here] = sums[column_chain[n_tiles + k]].astype(spread.dtype)

    scatter_phase(
        start, torus, col, transfers, order, split, n_col, grad_scale, spread, weight_parts, grad_preact, w_self,
        moved_in, weight_sums, arrived, self_grad, z_arrived, x_sums, z_sums,
        back_send, back_recv, *sems[10:],
    )
    for each in start.started:
        each.wait_send()


def finish_kernel(layer_in, moved_in, weight_sums, layer_out, grad_in, grad_self, grad_neigh):
    layer_out[...] = layer_in[...]
    grad_in[...] = lax.dot_general(
        row_order(moved_in.shape[0]), moved_in[...], (((0,), (0,)), ((), ())), preferred_element_type=jnp.float32
    ).astype(grad_in.dtype)
    rows = weight_sums.shape[1] // 2
    for c in range(weight_sums.shape[0]):
        grad_self[c * rows : (c + 1) * rows] = weight_sums[c, :rows].astype(grad_self.dtype)
        grad_neigh[c * rows : (c + 1) * rows] = weight_sums[c, rows:].astype(grad_neigh.dtype)


def array(dtype, *shape):
    return jax.ShapeDtypeStruct(shape, dtype)


def chains(keys, live, blocks):
    tiles = jnp.arange(keys.shape[0], dtype=jnp.int32)
    asked = jnp.concatenate([keys, jnp.arange(blocks, dtype=jnp.int32)])
    until = jnp.concatenate([tiles, jnp.full((blocks,), keys.shape[0], jnp.int32)])
    found = (tiles[None, :] < jnp.minimum(until[:, None], live)) & (keys[None, :] == asked[:, None])
    return jnp.max(jnp.where(found, tiles[None, :] + 1, 0), axis=1)


def shards(features, grad_out, degrees, w_self, w_neigh, bias, tile_slots, tile_count, tile_masks):
    size, width = features.shape
    n_row, n_col = lax.axis_size("row"), lax.axis_size("col")
    nx, nz = 4, n_row // 4
    ny, halves = n_col // 2, size // TILE
    split = [("xz", 0, 48), ("xz", 48, 48), ("zx", 96, 80), ("zx", 176, 80)]
    transfers, order = torus_plan(nx, nz, split)
    copies = len(transfers)
    bf16, f32, i32 = jnp.bfloat16, jnp.float32, jnp.int32
    dma = pltpu.SemaphoreType.DMA
    slots, live, masks = tile_slots[0, 0], tile_count[0, 0], tile_masks[0, 0]
    n_tiles = masks.shape[0]
    block_rows = n_col * halves
    block_columns = n_row * halves
    row_chain = chains(slots % block_rows, live, block_rows)
    column_chain = chains(slots // block_rows, live, block_columns)
    grad_scale = 1.0 / math.sqrt(size * n_row * n_col)
    grad_rows = 2 * width // n_col
    z_rows = grad_rows // nz
    others = n_col - 1
    y_copies = (ny - 1) * halves

    layer_in, moved_in, weight_sums = pl.pallas_call(
        functools.partial(layer_kernel, transfers, order, split, nx, nz, n_col, grad_scale),
        name="layer",
        out_shape=(
            array(bf16, size, width),
            array(bf16, size, width),
            array(bf16, n_col, grad_rows, width),
        ),
        in_specs=[SMEM] * 3 + [ANY] * 7,
        out_specs=(VMEM, VMEM, VMEM),
        scratch_shapes=[
            pltpu.VMEM((size, width), bf16),
            pltpu.VMEM((size, width), bf16),
            pltpu.VMEM((1, size), i32),
            pltpu.VMEM((width, width), bf16),
            pltpu.VMEM((width, width), bf16),
            pltpu.VMEM((1, width), f32),
            pltpu.VMEM(masks.shape, i32),
            pltpu.VMEM((size, width), bf16),
            pltpu.VMEM((n_row, size, width), bf16),
            pltpu.VMEM((n_tiles + 1, TILE, width), f32),
            pltpu.VMEM((block_rows, TILE, width), bf16),
            pltpu.VMEM((size, width), bf16),
            pltpu.VMEM((block_rows, TILE, width), bf16),
            pltpu.VMEM((nz, z_rows, width), f32),
            pltpu.VMEM((n_row, size, width), bf16),
            pltpu.VMEM((size, width), f32),
            pltpu.VMEM((size, width), f32),
            pltpu.VMEM((ny, halves, TILE, width), bf16),
            pltpu.VMEM((ny - 1, halves, TILE, width), bf16),
            pltpu.VMEM((ny - 1, halves, TILE, width), bf16),
            pltpu.VMEM((halves, TILE, width), f32),
            pltpu.VMEM((halves, TILE, width), bf16),
            pltpu.VMEM((size, width), bf16),
            pltpu.VMEM((n_col, grad_rows, width), bf16),
            pltpu.VMEM((others, grad_rows, width), bf16),
            pltpu.VMEM((copies, max(part[2] for part in split), width), bf16),
            pltpu.VMEM((size, width), f32),
            pltpu.VMEM((nz - 1, z_rows, width), f32),
            pltpu.VMEM((nx, z_rows, width), f32),
            pltpu.VMEM((nz, z_rows, width), f32),
            dma((7,)),
            dma,
        ]
        + [dma((copies,))] * 4
        + [dma((halves,))]
        + [dma((ny * halves,))] * 2
        + [dma((y_copies,))] * 4
        + [dma((ny * halves,))] * 2
        + [dma((others,))] * 2
        + [dma((nz - 1,))] * 2
        + [dma((nx - 1,))] * 2
        + [dma((nz - 1,))] * 2
        + [dma((others,))] * 2,
        compiler_params=pltpu.CompilerParams(
            collective_id=0, has_side_effects=True, vmem_limit_bytes=58 << 20
        ),
    )(
        slots,
        row_chain,
        column_chain,
        features,
        grad_out,
        degrees[None, :],
        w_self,
        w_neigh,
        bias[None, :],
        masks,
    )

    return pl.pallas_call(
        finish_kernel,
        name="finish",
        out_shape=(
            array(bf16, size, width),
            array(bf16, size, width),
            array(f32, width, width),
            array(f32, width, width),
        ),
        in_specs=[VMEM] * 3,
        out_specs=(VMEM,) * 4,
        compiler_params=pltpu.CompilerParams(vmem_limit_bytes=8 << 20),
    )(layer_in, moved_in, weight_sums)


def solution(mesh):
    placed = (
        P(("row", "col"), None),
        P(("row", "col"), None),
        P(("row", "col")),
        P(),
        P(),
        P(),
        P("row", "col", None),
        P("row", "col"),
        P("row", "col", None, None, None),
    )
    return jax.shard_map(
        shards,
        mesh=mesh,
        in_specs=placed,
        out_specs=(P(("row", "col"), None), P(("row", "col"), None), P(), P()),
        check_vma=False,
    )
```

time: 110 us -> 111 us (level)
  Pallas kernels: 107 us -> 103 us
  other arithmetic: 0 us -> 3.59 us
  local copies, waits for them, and re-layouts: 0.95 us -> 2.76 us
    pallas_call x5 -> x1, Pallas kernels: 106 us -> 102 us  [shards(): pl.pallas_call(functools.partial(layer_kernel, transfers, order, split, n...]
    unnamed x18 -> x6, local copies, waits for them, and re-layouts: 0.95 us -> 2.75 us
    reduce_max x0 -> x2, other arithmetic: none -> 1.38 us  [chains(): return jnp.max(jnp.where(found, tiles[None, :] + 1, 0), axis=1)]
    min x0 -> x2, other arithmetic: none -> 1.37 us  [chains(): jnp.minimum(until[:, None], live)]
where the time goes in v4:
time: 111 us; the launch traced here: 110 us
  Pallas kernels  103 us (93%)
  other arithmetic  3.59 us (3%)
  local copies, waits for them, and re-layouts  2.76 us (2%)
  between operations  1.31 us (1%)
    pallas_call x1, Pallas kernels, shards(): pl.pallas_call(functools.partial(layer_kernel, transfers, order, split, n...  102 us
    unnamed x6, local copies, waits for them, and re-layouts  2.75 us

profile of v4, /device:TPU:8, one launch (start us, length us, event | category | flops | bytes accessed | tf_op | source)
XLA Modules:
  0.0 110.3 jit_solution(543474817176307072)
XLA Ops:
  1.3 0.7 broadcast_minimum_fusion.1
  2.0 0.7 broadcast_minimum_fusion
  2.7 0.7 and_select_fusion
  3.4 0.1 pad_add_fusion.1
  3.4 0.7 select_reduce_fusion.column_chain
  4.1 0.1 pad_add_fusion
  4.2 0.7 select_reduce_fusion.1.row_chain
  4.9 101.6 %layer.1 = (bf16[256,256]{1,0:T(8,128)(2,1)}, bf16[256,256]{1,0:T(8,128)(2,1)}, bf16[8,64,256]{2,1,0:T(8,128)(2,1)}) custom-call(s32[176]{0:T(256)} %bitcast.9, s32[192]{0:T(256)} %select_reduce_fusion.1.row_chain, s32[240]{0:T(256)} %select_reduce_fusion.column_chain, bf16[256,256]{1,0:T(8,128)(2,1)} %features_in.1, bf16[256,256]{1,0:T(8,128)(2,1)} %grad_out_in.1, ...), custom_call_target="tpu_custom_call" | custom-call | tf_op jit(solution)/shard_map/layer/pallas_call | solution.py:506
  106.5 0.0 copy-start
  106.5 0.9 copy-done
  107.5 0.0 copy-start.1
  107.5 0.9 copy-done.1
  108.4 0.0 copy-start.2
  108.4 0.9 copy-done.2
  109.3 1.0 finish.1
  (2 shorter events, 0.0 us)
Async XLA Ops:
  106.5 1.0 copy-start
  107.5 0.9 copy-start.1
  108.4 0.9 copy-start.2

commit v5 on v4

--- a/solution.py
+++ b/solution.py
@@ -147,11 +147,29 @@
     )
 
 
-def chain_tiles(slots, before, masks, sums, product):
+def write_chains(slots_row, live, block_rows, n_tiles, chains):
+    lanes = chains.shape[1]
+    asked_slot = jnp.concatenate(
+        [slots_row[...], jnp.zeros((1, lanes - n_tiles), jnp.int32)], axis=1
+    )
+    place = lax.broadcasted_iota(jnp.int32, (1, lanes), 1)
+    tile = lax.broadcasted_iota(jnp.int32, (lanes, lanes), 0)
+    slot = jnp.broadcast_to(asked_slot, (lanes, lanes)).T
+    until = jnp.minimum(jnp.where(place < n_tiles, place, n_tiles), live)
+    shift = block_rows.bit_length() - 1
+    for k in range(2):
+        key = slot & (block_rows - 1) if k == 0 else slot >> shift
+        asked = asked_slot & (block_rows - 1) if k == 0 else asked_slot >> shift
+        asked = jnp.where(place < n_tiles, asked, place - n_tiles)
+        found = jnp.where((tile < until) & (key == asked), tile + 1, 0)
+        chains[k : k + 1] = jnp.max(found, axis=0, keepdims=True)
+
+
+def chain_tiles(slots, before, which, masks, sums, product):
     def group(index, _):
         for u in range(UNROLL):
             tile = index * UNROLL + u
-            sums[tile + 1] = sums[before[tile]] + product(slots[tile], unpack(masks[tile]))
+            sums[tile + 1] = sums[before[which, tile]] + product(slots[tile], unpack(masks[tile]))
         return 0
 
     lax.fori_loop(0, masks.shape[0] // UNROLL, group, 0)
@@ -249,7 +267,7 @@
 
 
 def scatter_phase(
-    start, torus, col, transfers, order, split, n_col, grad_scale, partial, weight_parts, grad_preact, w_self,
+    start, torus, col, transfers, order, split, n_col, grad_scale, partial, round_owner, weight_parts, grad_preact, w_self,
     moved_in, weight_sums, arrived, self_grad, z_arrived, x_sums, z_sums,
     send_sem, recv_sem, z_send, z_recv, x_send, x_recv, zz_send, zz_recv, cc_send, cc_recv,
 ):
@@ -337,8 +355,12 @@
     inner = sum(1 for _, brought, carried in order if brought and carried)
     stages = {inner * at // 100: step for at, step in zip(STAGES, steps)}
     seen = 0
+    rounded = set()
     for node, brought, carried in reversed(order[2 * n_parts :]):
         begin = split[node[0]][1]
+        if node[1:] not in rounded:
+            rounded.add(node[1:])
+            round_owner(torus.row(*node[1:]))
         if carried:
             if seen in stages:
                 pending = stages[seen](pending)
@@ -358,6 +380,7 @@
                 source = partial.at[torus.row(node[1], node[2]), pl.ds(first, count)]
             sent[index] = carry(index, source)
 
+    round_owner(torus.row(0, 0))
     sums = []
     for (node, _, first_carried), (_, _, carried) in zip(order[:n_parts], order[n_parts:]):
         sums.append((split[node[0]][1], sum_of(node, first_carried + carried)))
@@ -369,14 +392,14 @@
 
 def layer_kernel(
     transfers, order, split, nx, nz, n_col, grad_scale,
-    slots, row_chain, column_chain,
+    slots, live, slots_in,
     features_in, grad_out_in, degrees_in, w_self_in, w_neigh_in, bias_in, masks_in,
     layer_out, moved_in, weight_sums,
-    features, grad_out, degrees, w_self, w_neigh, bias, masks,
+    slots_row, features, grad_out, degrees, w_self, w_neigh, bias, masks,
     own, panel, sums, partial, grad_preact, upward_rows, weight_parts, spread,
     own_part, scale, from_sibling, joined, y_arrived, own_sum, upward, mean_rows, parts, parts_arrived,
     arrived, self_grad, z_arrived, x_sums, z_sums,
-    load_sem, own_sem, ring_send, ring_recv, back_send, back_recv, keep_sem, *sems,
+    chains, before, load_sem, own_sem, chain_sem, ring_send, ring_recv, back_send, back_recv, keep_sem, *sems,
 ):
     torus = Torus(nx, nz)
     col = lax.axis_index("col")
@@ -386,6 +409,7 @@
         for k, (source, target) in enumerate(
             (
                 (features_in, features),
+                (slots_in, slots_row),
                 (w_self_in, w_self),
                 (degrees_in, degrees),
                 (bias_in, bias),
@@ -412,8 +436,13 @@
 
     roots = 2 * len(split)
     sent = gather_phase(start, torus, transfers, order[:roots], own, panel, ring_send, ring_recv, {})
+    n_tiles, block_rows = masks.shape[0], partial.shape[0]
+    loads[1].wait()
+    write_chains(slots_row, live[0], block_rows, n_tiles, chains)
+    tables = pltpu.make_async_copy(chains, before, chain_sem)
+    tables.start()
     size, width = features.shape
-    for each in loads[1:]:
+    for each in loads[2:]:
         each.wait()
     scale[...] = jnp.broadcast_to(degrees[...].astype(jnp.float32), (width, size)).T
     own_part[...] = bias[...] + jnp.dot(
@@ -422,8 +451,8 @@
     sums[0] = jnp.zeros(sums.shape[1:], sums.dtype)
     gather_phase(start, torus, transfers, order[roots:], own, panel, ring_send, ring_recv, sent)
     keep.wait()
-
-    n_tiles, block_rows = masks.shape[0], partial.shape[0]
+    tables.wait()
+
     in_row = size // TILE
 
     def aggregate(slot, bits):
@@ -431,9 +460,9 @@
         source = panel[lax.div(block, in_row), pl.ds(lax.rem(block, in_row) * TILE, TILE)]
         return lax.dot_general(bits, source, (((0,), (0,)), ((), ())), preferred_element_type=jnp.float32)
 
-    chain_tiles(slots, row_chain, masks, sums, aggregate)
+    chain_tiles(slots, before, 0, masks, sums, aggregate)
     for k in range(block_rows):
-        partial[k] = sums[row_chain[n_tiles + k]].astype(partial.dtype)
+        partial[k] = sums[before[0, n_tiles + k]].astype(partial.dtype)
 
     middle_phase(
         start, col, partial, features, grad_out, w_neigh, layer_out, grad_preact, upward_rows, weight_parts,
@@ -444,13 +473,15 @@
     def spread_tile(slot, bits):
         return jnp.dot(bits, upward_rows[lax.rem(slot, block_rows)], preferred_element_type=jnp.float32)
 
-    chain_tiles(slots, column_chain, masks, sums, spread_tile)
-    for k in range(spread.shape[0] * in_row):
-        here = slice(k % in_row * TILE, (k % in_row + 1) * TILE)
-        spread[k // in_row, here] = sums[column_chain[n_tiles + k]].astype(spread.dtype)
+    chain_tiles(slots, before, 1, masks, sums, spread_tile)
+
+    def round_owner(owner):
+        for k in range(in_row):
+            last = before[1, n_tiles + owner * in_row + k]
+            spread[owner, k * TILE : (k + 1) * TILE] = sums[last].astype(spread.dtype)
 
     scatter_phase(
-        start, torus, col, transfers, order, split, n_col, grad_scale, spread, weight_parts, grad_preact, w_self,
+        start, torus, col, transfers, order, split, n_col, grad_scale, spread, round_owner, weight_parts, grad_preact, w_self,
         moved_in, weight_sums, arrived, self_grad, z_arrived, x_sums, z_sums,
         back_send, back_recv, *sems[10:],
     )
@@ -471,14 +502,6 @@
 
 def array(dtype, *shape):
     return jax.ShapeDtypeStruct(shape, dtype)
-
-
-def chains(keys, live, blocks):
-    tiles = jnp.arange(keys.shape[0], dtype=jnp.int32)
-    asked = jnp.concatenate([keys, jnp.arange(blocks, dtype=jnp.int32)])
-    until = jnp.concatenate([tiles, jnp.full((blocks,), keys.shape[0], jnp.int32)])
-    found = (tiles[None, :] < jnp.minimum(until[:, None], live)) & (keys[None, :] == asked[:, None])
-    return jnp.max(jnp.where(found, tiles[None, :] + 1, 0), axis=1)
 
 
 def shards(features, grad_out, degrees, w_self, w_neigh, bias, tile_slots, tile_count, tile_masks):
@@ -491,12 +514,11 @@
     copies = len(transfers)
     bf16, f32, i32 = jnp.bfloat16, jnp.float32, jnp.int32
     dma = pltpu.SemaphoreType.DMA
-    slots, live, masks = tile_slots[0, 0], tile_count[0, 0], tile_masks[0, 0]
+    slots, live, masks = tile_slots[0, 0], tile_count[0], tile_masks[0, 0]
     n_tiles = masks.shape[0]
     block_rows = n_col * halves
     block_columns = n_row * halves
-    row_chain = chains(slots % block_rows, live, block_rows)
-    column_chain = chains(slots // block_rows, live, block_columns)
+    places = -(-(n_tiles + max(block_rows, block_columns)) // TILE) * TILE
     grad_scale = 1.0 / math.sqrt(size * n_row * n_col)
     grad_rows = 2 * width // n_col
     z_rows = grad_rows // nz
@@ -511,9 +533,10 @@
             array(bf16, size, width),
             array(bf16, n_col, grad_rows, width),
         ),
-        in_specs=[SMEM] * 3 + [ANY] * 7,
+        in_specs=[SMEM, SMEM] + [ANY] * 8,
         out_specs=(VMEM, VMEM, VMEM),
         scratch_shapes=[
+            pltpu.VMEM((1, n_tiles), i32),
             pltpu.VMEM((size, width), bf16),
             pltpu.VMEM((size, width), bf16),
             pltpu.VMEM((1, size), i32),
@@ -544,7 +567,10 @@
             pltpu.VMEM((nz - 1, z_rows, width), f32),
             pltpu.VMEM((nx, z_rows, width), f32),
             pltpu.VMEM((nz, z_rows, width), f32),
-            dma((7,)),
+            pltpu.VMEM((2, places), i32),
+            pltpu.SMEM((2, places), i32),
+            dma((8,)),
+            dma,
             dma,
         ]
         + [dma((copies,))] * 4
@@ -562,8 +588,8 @@
         ),
     )(
         slots,
-        row_chain,
-        column_chain,
+        live,
+        slots[None, :],
         features,
         grad_out,
         degrees[None, :],
@@ -584,7 +610,7 @@
         ),
         in_specs=[VMEM] * 3,
         out_specs=(VMEM,) * 4,
-        compiler_params=pltpu.CompilerParams(vmem_limit_bytes=8 << 20),
+        compiler_params=pltpu.CompilerParams(vmem_limit_bytes=58 << 20),
     )(layer_in, moved_in, weight_sums)
 
 

time: 111 us -> 105 us (0.946)
  other arithmetic: 3.59 us -> 0 us
  local copies, waits for them, and re-layouts: 2.76 us -> 0 us
    unnamed x6 -> x0, local copies, waits for them, and re-layouts: 2.75 us -> none
    reduce_max x2 -> x0, other arithmetic: 1.38 us -> none  [chains(): return jnp.max(jnp.where(found, tiles[None, :] + 1, 0), axis=1)]
    min x2 -> x0, other arithmetic: 1.37 us -> none  [chains(): jnp.minimum(until[:, None], live)]
where the time goes in v5:
time: 105 us
  Pallas kernels  104 us (99%)
  between operations  1.29 us (1%)
    pallas_call x1, Pallas kernels, shards(): pl.pallas_call(functools.partial(layer_kernel, transfers, order, split, n...  101 us

profile of v5, /device:TPU:8, one launch (start us, length us, event | category | flops | bytes accessed | tf_op | source)
XLA Modules:
  0.0 104.9 jit_solution(6962253786761485542)
XLA Ops:
  1.3 101.5 %layer.1 = (bf16[256,256]{1,0:T(8,128)(2,1)}, bf16[256,256]{1,0:T(8,128)(2,1)}, bf16[8,64,256]{2,1,0:T(8,128)(2,1)}) custom-call(s32[176]{0:T(256)} %bitcast.8, s32[1]{0:T(128)} %bitcast.6.live, s32[1,176]{1,0:T(1,128)} %bitcast.9, bf16[256,256]{1,0:T(8,128)(2,1)} %features_in.1, bf16[256,256]{1,0:T(8,128)(2,1)} %grad_out_in.1, s32[1,256]{1,0:T(1,128)} %bitcast.10, ...), custom_call_target="tpu_custom_call" | custom-call | tf_op jit(solution)/shard_map/layer/pallas_call | solution.py:528
  102.8 2.1 %finish.1 = (bf16[256,256]{1,0:T(8,128)(2,1)}, bf16[256,256]{1,0:T(8,128)(2,1)}, f32[256,256]{1,0:T(8,128)}, f32[256,256]{1,0:T(8,128)}) custom-call(bf16[256,256]{1,0:T(8,128)(2,1)} %get-tuple-element.7.layer_in, bf16[256,256]{1,0:T(8,128)(2,1)} %get-tuple-element.8.moved_in, bf16[8,64,256]{2,1,0:T(8,128)(2,1)} %get-tuple-element.9.weight_sums), custom_call_target="tpu_custom_call" | custom-call | tf_op jit(solution)/shard_map/finish/pallas_call | solution.py:602

commit v6 on v5

--- a/solution.py
+++ b/solution.py
@@ -14,7 +14,7 @@
 VMEM = pl.BlockSpec(memory_space=pltpu.VMEM)
 ANY = pl.BlockSpec(memory_space=pl.ANY)
 TILE = 128
-UNROLL = 16
+UNROLL = 22
 STAGES = (0, 2, 18, 38, 58)
 
 
@@ -489,8 +489,9 @@
         each.wait_send()
 
 
-def finish_kernel(layer_in, moved_in, weight_sums, layer_out, grad_in, grad_self, grad_neigh):
-    layer_out[...] = layer_in[...]
+def finish_kernel(layer_in, moved_in, weight_sums, layer_out, grad_in, grad_self, grad_neigh, layer_sem):
+    hand_on = pltpu.make_async_copy(layer_in, layer_out, layer_sem)
+    hand_on.start()
     grad_in[...] = lax.dot_general(
         row_order(moved_in.shape[0]), moved_in[...], (((0,), (0,)), ((), ())), preferred_element_type=jnp.float32
     ).astype(grad_in.dtype)
@@ -498,6 +499,7 @@
     for c in range(weight_sums.shape[0]):
         grad_self[c * rows : (c + 1) * rows] = weight_sums[c, :rows].astype(grad_self.dtype)
         grad_neigh[c * rows : (c + 1) * rows] = weight_sums[c, rows:].astype(grad_neigh.dtype)
+    hand_on.wait()
 
 
 def array(dtype, *shape):
@@ -608,8 +610,9 @@
             array(f32, width, width),
             array(f32, width, width),
         ),
-        in_specs=[VMEM] * 3,
-        out_specs=(VMEM,) * 4,
+        in_specs=[ANY, VMEM, VMEM],
+        out_specs=(ANY, VMEM, VMEM, VMEM),
+        scratch_shapes=[pltpu.SemaphoreType.DMA],
         compiler_params=pltpu.CompilerParams(vmem_limit_bytes=58 << 20),
     )(layer_in, moved_in, weight_sums)
 

time: 105 us -> 109 us (1.038)
  Pallas kernels: 104 us -> 107 us
    pallas_call x1, Pallas kernels: 2.1 us -> 6.93 us  [shards(): pl.pallas_call(finish_kernel, name='finish', out_shape=(array(bf16, size,...]
    pallas_call x1, Pallas kernels: 101 us -> 100 us  [shards(): pl.pallas_call(functools.partial(layer_kernel, transfers, order, split, n...]
where the time goes in v6:
time: 109 us
  Pallas kernels  107 us (98%)
  between operations  1.29 us (1%)
    pallas_call x1, Pallas kernels, shards(): pl.pallas_call(functools.partial(layer_kernel, transfers, order, split, n...  100 us
    pallas_call x1, Pallas kernels, shards(): pl.pallas_call(finish_kernel, name='finish', out_shape=(array(bf16, size,...  6.93 us

profile of v6, /device:TPU:8, one launch (start us, length us, event | category | flops | bytes accessed | tf_op | source)
XLA Modules:
  0.0 108.5 jit_solution(34824366404016923)
XLA Ops:
  1.3 100.3 %layer.1 = (bf16[256,256]{1,0:T(8,128)(2,1)}, bf16[256,256]{1,0:T(8,128)(2,1)}, bf16[8,64,256]{2,1,0:T(8,128)(2,1)}) custom-call(s32[176]{0:T(256)} %bitcast.8, s32[1]{0:T(128)} %bitcast.6.live, s32[1,176]{1,0:T(1,128)} %bitcast.9, bf16[256,256]{1,0:T(8,128)(2,1)} %features_in.1, bf16[256,256]{1,0:T(8,128)(2,1)} %grad_out_in.1, s32[1,256]{1,0:T(1,128)} %bitcast.10, ...), custom_call_target="tpu_custom_call" | custom-call | tf_op jit(solution)/shard_map/layer/pallas_call | solution.py:530
  101.6 6.9 %finish.1 = (bf16[256,256]{1,0:T(8,128)(2,1)}, bf16[256,256]{1,0:T(8,128)(2,1)}, f32[256,256]{1,0:T(8,128)}, f32[256,256]{1,0:T(8,128)}) custom-call(bf16[256,256]{1,0:T(8,128)(2,1)} %get-tuple-element.7.layer_in, bf16[256,256]{1,0:T(8,128)(2,1)} %get-tuple-element.8.moved_in, bf16[8,64,256]{2,1,0:T(8,128)(2,1)} %get-tuple-element.9.weight_sums), custom_call_target="tpu_custom_call" | custom-call | tf_op jit(solution)/shard_map/finish/pallas_call | solution.py:604
